TPU v7x, 128 devices: a whole 4x4x4 slice. The times are simulated.
128 devices in a mesh: blk: 32 (over z, y, core), sub: 4 (over x).
Axes of the slice: x: 4, y: 4, z: 4, core: 2. Of those that a mesh axis runs over, the one named last changes fastest.
Arguments:
- dynamics_profile_values: float32 [131072, 768], P(('blk', 'sub')), may hold values from -6 to 6
- parameterized_increments: float32 [131072, 768], P(('blk', 'sub')), may hold values from -4 to 4
- ground_exchange_rates: float32 [6, 131072], P(None, ('blk', 'sub')), may hold values from -6 to 6
- sunlit_indicator: int32 [131072], P(('blk', 'sub')), may hold values 0 or 1
- eddy_coefficient_scale: float32 [131072], P(('blk', 'sub')), may hold values from 0.05 to 100
- departing_profile_indices: int32 [128, 128, 8], P(('blk', 'sub')), may hold values from 0 to 1024, as said below
- arriving_parcel_places: int32 [128, 128, 8], P(('blk', 'sub')), may hold values from 0 to 1024, as said below
- resident_parcel_place: int32 [128, 1024], P(('blk', 'sub')), may hold values from 0 to 1024, as said below
- boundary_profile_indices: int32 [128, 2, 128], P(('blk', 'sub')), may hold values from 0 to 1023, as said below
Outputs:
- span_state: float32 [131072, 768], P(('blk', 'sub'))
- column_result: float32 [131072, 768], P(('blk', 'sub'))
Inputs may be any that keep to these rules, and one draw needn't show every extreme that they name: departing_profile_indices[n, p] names distinct own columns of device n that go to device p, then 1024 in the empty slots; no column is named twice for n and none stays named for p = n. The number of columns n sends to (n + o) mod 128 is between 1 and 8 for o ≠ 0, depends only on o, is 8 for some o and 1 for another. arriving_parcel_places[p, n, c] is the span position on device p of the column in departing_profile_indices[n, p, c], or 1024 exactly where that slot is empty. resident_parcel_place[n, j] is the span position on device n of its own column j if that column stays, else 1024 (exactly for the columns named in departing_profile_indices[n]); with arriving_parcel_places, every span position of every device is filled exactly once. boundary_profile_indices[n] names 256 distinct columns of device n; left point k of device b * 4 + s is the same grid point as right point k of device ((b - 1) mod 32) * 4 + s.
All inputs are finite; a program needn't handle non-finite values. No bound on the sum of `sunlit_indicator` on one device may be relied on, other than what follows from the above.
Results may differ from a plain program's by a relative error of at most 0.000066.
Values sent between devices are 32-bit elements; how exact they have to be, the bound alone decides.
No kernel may reach another device: no remote copies, remote signals or barrier semaphores. Data moves between devices by JAX's collectives and lax.ppermute only.
A program may use at most 128 MiB of HBM per device.

v0:
```python
import functools

import jax
import jax.numpy as jnp
from jax import lax
from jax.experimental import pallas as pl
from jax.experimental.pallas import tpu as pltpu
from jax.sharding import PartitionSpec as P

FIELDS = 6
LEV = 128
COLS = 1024
PEERS = 128
CAP = 8
EDGE = 128
ROW = 7
DUMP = COLS
ROWS_ALLOC = 7176
X_PART = CAP * FIELDS
MESSAGE = X_PART + CAP * ROW
GROUP = 137
VMEM_LIMIT = 60 * 2**20
HEAT = (0, 1, 4, 5)
RICHARDSON = {0: 0, 2: 1, 3: 2}


def to_tiles(rows):
    return rows.reshape(COLS // 8, 8, FIELDS, LEV).transpose(0, 2, 1, 3).reshape(COLS * FIELDS, LEV)


def from_tiles(tiles):
    return tiles.reshape(COLS // 8, FIELDS, 8, LEV).transpose(0, 2, 1, 3).reshape(COLS, FIELDS * LEV)


def spread_rows(tiles, rows):
    def body(t, carry):
        for f in range(FIELDS):
            rows[pl.ds(t * 8 * ROW + f, 8, stride=ROW), :] = tiles[pl.ds(t * 48 + f * 8, 8), :]
        return carry

    lax.fori_loop(0, COLS // 8, body, 0, unroll=4)


def spread_scalars(scalars, rows):
    for g in range(8):
        part = scalars[:, g * 128 : (g + 1) * 128]
        square = jnp.concatenate([part] * 16, axis=0).T
        for i in range(16):
            rows[pl.ds((g * 128 + i * 8) * ROW + FIELDS, 8, stride=ROW), :] = square[i * 8 : (i + 1) * 8]


def pack_kernel(departing, arriving, x, inc, scalars, send, x_rows, inc_rows):
    spread_rows(x, x_rows)
    spread_rows(inc, inc_rows)
    spread_scalars(scalars, inc_rows)

    def body(p, carry):
        for c in range(CAP):
            j = jnp.minimum(departing[p * CAP + c], COLS - 1)
            send[pl.ds(p * MESSAGE + c * FIELDS, FIELDS), :] = x_rows[pl.ds(j * ROW, FIELDS), :]
        for c in range(CAP):
            q = jnp.minimum(arriving[p * CAP + c], COLS - 1)
            send[pl.ds(p * MESSAGE + X_PART + c * ROW, ROW), :] = inc_rows[pl.ds(q * ROW, ROW), :]
        return carry

    lax.fori_loop(0, PEERS, body, 0)


def resident_kernel(staying, x, inc, scalars, span_x, block_inc, x_rows, inc_rows):
    spread_rows(x, x_rows)
    spread_rows(inc, inc_rows)
    spread_scalars(scalars, inc_rows)

    def body(t, carry):
        for i in range(8):
            j = t * 8 + i
            q = staying[j]
            span_x[pl.ds(q * ROW, FIELDS), :] = x_rows[pl.ds(j * ROW, FIELDS), :]
            source = jnp.minimum(q, COLS - 1)
            block_inc[pl.ds(j * ROW, ROW), :] = inc_rows[pl.ds(source * ROW, ROW), :]
        return carry

    lax.fori_loop(0, COLS // 8, body, 0)


def tile_block(tiles, g, f):
    return jnp.concatenate(
        [tiles[pl.ds((g * 16 + i) * 48 + f * 8, 8), :] for i in range(16)], axis=0
    )


def row_block(rows, g, f):
    return jnp.concatenate(
        [rows[pl.ds((g * 128 + i * 8) * ROW + f, 8, stride=ROW), :] for i in range(16)], axis=0
    )


def transpose_in(load_x, load_inc, wind, right):
    def body(g, carry):
        for f in range(FIELDS):
            x = load_x(g, f)
            if f in RICHARDSON:
                wind[RICHARDSON[f], pl.ds(g * GROUP, LEV), :] = x.T
            right[f, pl.ds(g * GROUP, LEV), :] = (x + load_inc(g, f)).T
        return carry

    lax.fori_loop(0, 8, body, 0)


def transpose_out(right, tiles):
    def body(g, carry):
        for f in range(FIELDS):
            block = right[f, pl.ds(g * GROUP, LEV), :].T
            for i in range(16):
                tiles[pl.ds((g * 16 + i) * 48 + f * 8, 8), :] = block[i * 8 : (i + 1) * 8]
        return carry

    lax.fori_loop(0, 8, body, 0)


def level(ref, f, k):
    return ref[f, pl.ds(k, 8, stride=GROUP), :]


def put_level(ref, f, k, value):
    ref[f, pl.ds(k, 8, stride=GROUP), :] = value


def interface_weight(eddy, upper, lower):
    lapse = upper[0] - lower[0]
    u = upper[1] - lower[1]
    v = upper[2] - lower[2]
    shear = u * u + v * v + 0.1
    unstable = lapse < 0.0
    stable_root = shear + 10.0 * lapse
    top = jnp.where(unstable, shear - 8.0 * lapse, shear * shear)
    bottom = jnp.where(unstable, shear - lapse, stable_root * stable_root)
    wind = eddy * (top / bottom)
    return (1.35 * wind, wind)


def solve(wind, right, factor, forcing, eddy):
    for f in range(FIELDS):
        put_level(right, f, LEV - 1, level(right, f, LEV - 1) + forcing[f])

    def state(k):
        return [level(wind, i, k) for i in range(3)]

    zero = jnp.zeros((8, 128), jnp.float32)

    def eliminate(i, carry):
        excess, moved, above, below = carry
        ks = (i, LEV - 1 - i)
        inner = (state(i + 1), state(LEV - 2 - i))
        weights = (
            interface_weight(eddy, above, inner[0]),
            interface_weight(eddy, inner[1], below),
        )
        new_excess = [[], []]
        new_moved = [[], []]
        for side in range(2):
            ratio = []
            inverse = []
            for m in range(2):
                base = 1.0 + excess[side][m]
                inv = 1.0 / (base + weights[side][m])
                out = weights[side][m] * inv
                factor[side, m, i] = out
                ratio.append(out)
                inverse.append(inv)
                new_excess[side].append(base * out)
            for f in range(FIELDS):
                m = 0 if f in HEAT else 1
                z = level(right, f, ks[side]) + moved[side][f]
                put_level(right, f, ks[side], z * inverse[m])
                new_moved[side].append(z * ratio[m])
        return new_excess, new_moved, inner[0], inner[1]

    start = ([[zero] * 2] * 2, [[zero] * FIELDS] * 2, state(0), state(LEV - 1))
    half = LEV // 2
    excess, moved, above, below = lax.fori_loop(0, half - 1, eliminate, start, unroll=3)
    weight = interface_weight(eddy, above, below)
    solved = [[], []]
    for f in range(FIELDS):
        m = 0 if f in HEAT else 1
        w = weight[m]
        a = 1.0 + excess[0][m]
        b = 1.0 + excess[1][m]
        inv = 1.0 / (a * b + w * (a + b))
        za = level(right, f, half - 1) + moved[0][f]
        zb = level(right, f, half) + moved[1][f]
        ya = ((b + w) * za + w * zb) * inv
        yb = ((a + w) * zb + w * za) * inv
        put_level(right, f, half - 1, ya)
        put_level(right, f, half, yb)
        solved[0].append(ya)
        solved[1].append(yb)

    def substitute(i, carry):
        step = half - 2 - i
        ks = (step, LEV - 1 - step)
        new = [[], []]
        for side in range(2):
            ratio = [factor[side, m, step] for m in range(2)]
            for f in range(FIELDS):
                m = 0 if f in HEAT else 1
                y = level(right, f, ks[side]) + ratio[m] * carry[side][f]
                put_level(right, f, ks[side], y)
                new[side].append(y)
        return new

    lax.fori_loop(0, half - 1, substitute, solved, unroll=3)


def finish_kernel(
    departing, arriving, edges, x, inc, forcing, eddy, recv, span_rows, block_rows,
    span_out, block_out, left_rows, right_rows, wind, right, factor, scalars,
):
    def land(p, carry):
        for c in range(CAP):
            q = arriving[p * CAP + c]
            span_rows[pl.ds(q * ROW, FIELDS), :] = recv[pl.ds(p * MESSAGE + c * FIELDS, FIELDS), :]
        for c in range(CAP):
            j = departing[p * CAP + c]
            block_rows[pl.ds(j * ROW, ROW), :] = recv[pl.ds(p * MESSAGE + X_PART + c * ROW, ROW), :]
        return carry

    lax.fori_loop(0, PEERS, land, 0)

    transpose_in(
        lambda g, f: tile_block(x, g, f), lambda g, f: row_block(block_rows, g, f), wind, right
    )
    for g in range(8):
        scalars[0, pl.ds(g * GROUP, LEV), :] = row_block(block_rows, g, FIELDS).T
    solve(
        wind, right, factor,
        [level(scalars, 0, f) for f in range(FIELDS)],
        level(scalars, 0, FIELDS),
    )
    transpose_out(right, block_out)

    def edge(k, carry):
        for side, out in ((0, left_rows), (1, right_rows)):
            j = edges[side * EDGE + k]
            base = (j >> 3) * 48 + (j & 7)
            out[pl.ds(k * FIELDS, FIELDS), :] = block_out[pl.ds(base, FIELDS, stride=8), :]
        return carry

    lax.fori_loop(0, EDGE, edge, 0, unroll=4)

    transpose_in(
        lambda g, f: row_block(span_rows, g, f), lambda g, f: tile_block(inc, g, f), wind, right
    )
    solve(wind, right, factor, [forcing[f] for f in range(FIELDS)], eddy[...])
    transpose_out(right, span_out)


def average_kernel(edges, column, own_left, own_right, far_left, far_right, out):
    out[...] = column[...]

    def body(k, carry):
        for side, own, far in ((0, own_left, far_left), (1, own_right, far_right)):
            j = edges[side * EDGE + k]
            base = (j >> 3) * 48 + (j & 7)
            rows = pl.ds(k * FIELDS, FIELDS)
            out[pl.ds(base, FIELDS, stride=8), :] = (own[rows, :] + far[rows, :]) * 0.5
        return carry

    lax.fori_loop(0, EDGE, body, 0, unroll=4)


def shape(*dims):
    return jax.ShapeDtypeStruct(dims, jnp.float32)


def in_smem():
    return pl.BlockSpec(memory_space=pltpu.SMEM)


def in_vmem():
    return pl.BlockSpec(memory_space=pltpu.VMEM)


def call(kernel, tables, arrays, out_shape, scratch=(), aliases={}, cost=None):
    return pl.pallas_call(
        kernel,
        out_shape=out_shape,
        in_specs=[in_smem()] * len(tables) + [in_vmem()] * len(arrays),
        out_specs=jax.tree.map(lambda _: in_vmem(), out_shape),
        scratch_shapes=list(scratch),
        input_output_aliases=aliases,
        compiler_params=pltpu.CompilerParams(vmem_limit_bytes=VMEM_LIMIT),
        cost_estimate=cost,
    )(*tables, *arrays)


def on_device(
    dynamics_profile_values,
    parameterized_increments,
    ground_exchange_rates,
    sunlit_indicator,
    eddy_coefficient_scale,
    departing_profile_indices,
    arriving_parcel_places,
    resident_parcel_place,
    boundary_profile_indices,
):
    departing = departing_profile_indices.reshape(-1)
    arriving = arriving_parcel_places.reshape(-1)
    staying = resident_parcel_place.reshape(-1)
    edges = boundary_profile_indices.reshape(-1)
    x = to_tiles(dynamics_profile_values)
    inc = to_tiles(parameterized_increments)
    forcing = ground_exchange_rates * (0.5 + sunlit_indicator.astype(jnp.float32))
    eddy = eddy_coefficient_scale
    scalars = jnp.concatenate([forcing, eddy[None], eddy[None]], axis=0)
    rows = pltpu.VMEM((ROWS_ALLOC, LEV), jnp.float32)

    send = call(
        pack_kernel, (departing, arriving), (x, inc, scalars),
        shape(PEERS * MESSAGE, LEV), (rows, rows),
    )
    recv = lax.all_to_all(
        send.reshape(PEERS, MESSAGE, LEV), ("blk", "sub"), split_axis=0, concat_axis=0, tiled=True
    ).reshape(PEERS * MESSAGE, LEV)
    span_rows, block_rows = call(
        resident_kernel, (staying,), (x, inc, scalars),
        (shape(ROWS_ALLOC, LEV), shape(ROWS_ALLOC, LEV)), (rows, rows),
        cost=pl.CostEstimate(flops=0, bytes_accessed=14 * 2**20, transcendentals=0),
    )
    transposed = functools.partial(pltpu.VMEM, dtype=jnp.float32)
    span_out, block_out, left_rows, right_rows = call(
        finish_kernel, (departing, arriving, edges),
        (x, inc, forcing.reshape(FIELDS, 8, LEV), eddy.reshape(8, LEV), recv, span_rows, block_rows),
        (shape(COLS * FIELDS, LEV), shape(COLS * FIELDS, LEV), shape(EDGE * FIELDS, LEV), shape(EDGE * FIELDS, LEV)),
        (
            transposed((3, 8 * GROUP, LEV)),
            transposed((FIELDS, 8 * GROUP, LEV)),
            transposed((2, 2, LEV // 2, 8, LEV)),
            transposed((1, 8 * GROUP, LEV)),
        ),
    )
    count = lax.axis_size("blk")
    far_left = lax.ppermute(right_rows, "blk", [(i, (i + 1) % count) for i in range(count)])
    far_right = lax.ppermute(left_rows, "blk", [((i + 1) % count, i) for i in range(count)])
    column = call(
        average_kernel, (edges,), (block_out, left_rows, right_rows, far_left, far_right),
        shape(COLS * FIELDS, LEV),
    )
    return from_tiles(span_out), from_tiles(column)


def solution(mesh):
    one = P(("blk", "sub"))
    placed = (one, one, P(None, ("blk", "sub")), one, one, one, one, one, one)
    return jax.shard_map(
        on_device, mesh=mesh, in_specs=placed, out_specs=(one, one), check_vma=False
    )
```

profile of v0, /device:TPU:0, one launch (start us, length us, event | category | flops | bytes accessed | tf_op | source)
XLA Modules:
  0.0 150.7 jit_solution(11077130070113588568)
XLA Ops:
  0.6 0.7 convert_add_fusion
  1.3 0.8 copy.11
  2.1 0.7 reshape.53.departing
  2.8 0.8 copy.12
  3.6 0.7 reshape.54.arriving
  4.2 0.8 broadcast_multiply_fusion
  5.0 1.4 pad_maximum_fusion.scalars
  6.4 10.3 %shard_map.104 = f32[13312,128]{1,0:T(8,128)} custom-call(s32[1024]{0:T(1024)} %reshape.53.departing, s32[1024]{0:T(1024)} %reshape.54.arriving, f32[6144,128]{1,0:T(8,128)} %bitcast.31, f32[6144,128]{1,0:T(8,128)} %bitcast.34, f32[8,1024]{1,0:T(8,128)} %pad_maximum_fusion.scalars), custom_call_target="tpu_custom_call" | custom-call | tf_op jit(solution)/shard_map/pallas_call | solution.py:285
  16.7 0.0 copy-start.2
  16.7 11.6 %all-to-all-start = ((f32[128,104,128]{2,1,0:T(8,128)}), f32[128,104,128]{2,1,0:T(8,128)}, u32[]{:S(2)}, u32[]{:S(2)}) async-start(f32[128,104,128]{2,1,0:T(8,128)} %bitcast.37), calls=%async_computation | async-start | bytes 13631488 | tf_op jit(solution)/shard_map/all_to_all | solution.py:323
  28.3 0.0 copy-done.2
  28.3 0.6 copy.15
  28.9 9.4 %shard_map.105 = (f32[7176,128]{1,0:T(8,128)}, f32[7176,128]{1,0:T(8,128)}) custom-call(s32[1024]{0:T(1024)} %bitcast.44, f32[6144,128]{1,0:T(8,128)} %bitcast.32, f32[6144,128]{1,0:T(8,128)} %bitcast.35, f32[8,1024]{1,0:T(8,128)} %pad_maximum_fusion.scalars), custom_call_target="tpu_custom_call" | custom-call | bytes 14680064 | tf_op jit(solution)/shard_map/pallas_call | solution.py:285
  38.4 72.3 %all-to-all-done = f32[128,104,128]{2,1,0:T(8,128)} async-done(((f32[128,104,128]{2,1,0:T(8,128)}), f32[128,104,128]{2,1,0:T(8,128)}, u32[]{:S(2)}, u32[]{:S(2)}) %all-to-all-start) | async-done | bytes 6815776 | tf_op jit(solution)/shard_map/all_to_all | solution.py:323
  110.7 23.1 %shard_map.106 = (f32[6144,128]{1,0:T(8,128)}, f32[6144,128]{1,0:T(8,128)}, f32[768,128]{1,0:T(8,128)}, f32[768,128]{1,0:T(8,128)}) custom-call(s32[1024]{0:T(1024)} %reshape.53.departing, s32[1024]{0:T(1024)} %reshape.54.arriving, s32[256]{0:T(256)} %bitcast.42, f32[6144,128]{1,0:T(8,128)} %bitcast.33, f32[6144,128]{1,0:T(8,128)} %bitcast.36, ...), custom_call_target="tpu_custom_call" | custom-call | tf_op jit(solution)/shard_map/pallas_call | solution.py:285
  133.8 0.6 collective-permute-start.1
  134.4 0.0 collective-permute-start
  134.4 5.6 %collective-permute-done.1.far_right = f32[768,128]{1,0:T(8,128)S(1)} collective-permute-done((f32[768,128]{1,0:T(8,128)}, f32[768,128]{1,0:T(8,128)S(1)}, u32[]{:S(2)}, u32[]{:S(2)}) %collective-permute-start.1) | collective-permute-done | bytes 393248 | tf_op jit(solution)/shard_map/ppermute | solution.py:345
  140.0 0.0 copy-start
  140.0 5.1 %collective-permute-done.far_left = f32[768,128]{1,0:T(8,128)S(1)} collective-permute-done((f32[768,128]{1,0:T(8,128)}, f32[768,128]{1,0:T(8,128)S(1)}, u32[]{:S(2)}, u32[]{:S(2)}) %collective-permute-start) | collective-permute-done | bytes 393248 | tf_op jit(solution)/shard_map/ppermute | solution.py:344
  145.1 0.0 copy-start.1
  145.1 0.0 copy-done
  145.1 0.7 copy-done.1
  145.9 4.9 %shard_map.107 = f32[6144,128]{1,0:T(8,128)} custom-call(s32[256]{0:T(256)} %bitcast.43, f32[6144,128]{1,0:T(8,128)} %get-tuple-element.11.column, f32[768,128]{1,0:T(8,128)} %get-tuple-element.12.own_left, f32[768,128]{1,0:T(8,128)} %get-tuple-element.13.own_right, f32[768,128]{1,0:T(8,128)} %copy-done.1, f32[768,128]{1,0:T(8,128)} %copy-done), custom_call_target="tpu_custom_call" | custom-call | tf_op jit(solution)/shard_map/pallas_call | solution.py:285
  (1 shorter events, 0.0 us)
Async XLA Ops:
  16.7 11.7 %copy-start.2 = (f32[6,1024]{1,0:T(8,128)S(1)}, f32[6,1024]{1,0:T(8,128)}, u32[]{:S(2)}) copy-start(f32[6,1024]{1,0:T(8,128)} %param.11) | copy-start | bytes 73732
  16.7 94.0 %all-to-all-start = ((f32[128,104,128]{2,1,0:T(8,128)}), f32[128,104,128]{2,1,0:T(8,128)}, u32[]{:S(2)}, u32[]{:S(2)}) async-start(f32[128,104,128]{2,1,0:T(8,128)} %bitcast.37), calls=%async_computation | async-start | bytes 13631488 | tf_op jit(solution)/shard_map/all_to_all | solution.py:323
  133.8 6.2 %collective-permute-start.1 = (f32[768,128]{1,0:T(8,128)}, f32[768,128]{1,0:T(8,128)S(1)}, u32[]{:S(2)}, u32[]{:S(2)}) collective-permute-start(f32[768,128]{1,0:T(8,128)} %get-tuple-element.12.own_left), channel_id=1, source_target_pairs={{4,0},{8,4},{12,8},{16,12},{20,16},{24,20},{28,24},{32,28},{36,32}... | collective-permute-start | bytes 1179656 | tf_op jit(solution)/shard_map/ppermute | solution.py:345
  134.4 10.7 %collective-permute-start = (f32[768,128]{1,0:T(8,128)}, f32[768,128]{1,0:T(8,128)S(1)}, u32[]{:S(2)}, u32[]{:S(2)}) collective-permute-start(f32[768,128]{1,0:T(8,128)} %get-tuple-element.13.own_right), channel_id=1, source_target_pairs={{0,4},{4,8},{8,12},{12,16},{16,20},{20,24},{24,28},{28,32},{32,36}... | collective-permute-start | bytes 1179656 | tf_op jit(solution)/shard_map/ppermute | solution.py:344
  140.0 5.1 %copy-start = (f32[768,128]{1,0:T(8,128)}, f32[768,128]{1,0:T(8,128)S(1)}, u32[]{:S(2)}) copy-start(f32[768,128]{1,0:T(8,128)S(1)} %collective-permute-done.1.far_right) | copy-start | bytes 1179652
  145.1 0.7 copy-start.1
where the time goes:
time: 151 us
  waiting for transfers between devices  83 us (55%)
  Pallas kernels  47.7 us (32%)
  starting transfers between devices  12.3 us (8%)
  local copies, waits for them, and re-layouts  4.27 us (3%)
  other arithmetic  2.85 us (2%)
    all_to_all x1, waiting for transfers between devices, on_device(): lax.all_to_all(send.reshape(PEERS, MESSAGE, LEV), ('blk', 'sub'), split_a...  72.3 us
    pallas_call x4, Pallas kernels, call(): pl.pallas_call(kernel, out_shape=out_shape, in_specs=[in_smem()] * len(ta...  47.7 us
    all_to_all x1, starting transfers between devices, on_device(): lax.all_to_all(send.reshape(PEERS, MESSAGE, LEV), ('blk', 'sub'), split_a...  11.6 us
    ppermute x1, waiting for transfers between devices, on_device(): lax.ppermute(left_rows, 'blk', [((i + 1) % count, i) for i in range(count)])  5.58 us
    ppermute x1, waiting for transfers between devices, on_device(): lax.ppermute(right_rows, 'blk', [(i, (i + 1) % count) for i in range(coun...  5.12 us
  transfers between devices with their start and end apart: 3, of which 3 were waited for; matrix products, arithmetic and copies ran while one was open for 0% of the time, Pallas kernels for 6%

commit v1 on v0

v1 whole, which is shorter than its diff:
```python
import jax
import jax.numpy as jnp
from jax import lax
from jax.experimental import pallas as pl
from jax.experimental.pallas import tpu as pltpu
from jax.sharding import PartitionSpec as P

FIELDS = 6
LEV = 128
COLS = 1024
PEERS = 128
CAP = 8
EDGE = 128
ROW = 7
DUMP = COLS
ROWS_ALLOC = 7176
X_PART = CAP * FIELDS
MESSAGE = X_PART + CAP * ROW
GROUP = 137
VMEM_LIMIT = 60 * 2**20
HEAT = (0, 1, 4, 5)
RICHARDSON = {0: 0, 2: 1, 3: 2}


def to_tiles(rows):
    return rows.reshape(COLS // 8, 8, FIELDS, LEV).transpose(0, 2, 1, 3).reshape(COLS * FIELDS, LEV)


def from_tiles(tiles):
    return tiles.reshape(COLS // 8, FIELDS, 8, LEV).transpose(0, 2, 1, 3).reshape(COLS, FIELDS * LEV)


def copy_chunks(pairs, sems, first):
    copies = [
        pltpu.make_async_copy(source, target, sems.at[first + i])
        for i, (source, target) in enumerate(pairs)
    ]
    for one in copies:
        one.start()
    return copies


def chunked(source, target, parts):
    size = source.shape[0] // parts
    return [
        (source.at[pl.ds(i * size, size)], target.at[pl.ds(i * size, size)]) for i in range(parts)
    ]


def spread_rows(tiles, rows, first, count):
    def body(t, carry):
        for f in range(FIELDS):
            rows[pl.ds(t * 8 * ROW + f, 8, stride=ROW), :] = tiles[pl.ds(t * 48 + f * 8, 8), :]
        return carry

    lax.fori_loop(first, first + count, body, 0, unroll=4)


def spread_scalars(rates, sunlit, eddy, rows):
    for g in range(8):
        lanes = pl.ds(g * 128, 128)
        one = pl.ds(g, 1)
        forcing = rates[:, lanes] * (0.5 + sunlit[one, :].astype(jnp.float32))
        part = jnp.concatenate([forcing, eddy[one, :], eddy[one, :]], axis=0)
        square = jnp.concatenate([part] * 16, axis=0).T
        for i in range(16):
            rows[pl.ds((g * 128 + i * 8) * ROW + FIELDS, 8, stride=ROW), :] = square[i * 8 : (i + 1) * 8]


def load_rows(x, inc, rates, sunlit, eddy, x_tiles, inc_tiles, x_rows, inc_rows, sems):
    parts = 4
    x_copies = copy_chunks(chunked(x, x_tiles, parts), sems, 0)
    inc_copies = copy_chunks(chunked(inc, inc_tiles, parts), sems, parts)
    spread_scalars(rates, sunlit, eddy, inc_rows)
    count = COLS // 8 // parts
    for copies, tiles, rows in ((x_copies, x_tiles, x_rows), (inc_copies, inc_tiles, inc_rows)):
        for i, one in enumerate(copies):
            one.wait()
            spread_rows(tiles, rows, i * count, count)


def pack_kernel(
    departing, arriving, x, inc, rates, sunlit, eddy, send,
    x_tiles, inc_tiles, x_rows, inc_rows, packed, sems,
):
    load_rows(x, inc, rates, sunlit, eddy, x_tiles, inc_tiles, x_rows, inc_rows, sems)

    def body(p, carry):
        for c in range(CAP):
            j = jnp.minimum(departing[c, p], COLS - 1)
            packed[pl.ds(p * MESSAGE + c * FIELDS, FIELDS), :] = x_rows[pl.ds(j * ROW, FIELDS), :]
        for c in range(CAP):
            q = jnp.minimum(arriving[c, p], COLS - 1)
            packed[pl.ds(p * MESSAGE + X_PART + c * ROW, ROW), :] = inc_rows[pl.ds(q * ROW, ROW), :]
        return carry

    parts = 8
    step = PEERS // parts
    copies = []
    for i, pair in enumerate(chunked(packed, send, parts)):
        lax.fori_loop(i * step, (i + 1) * step, body, 0)
        copies += copy_chunks([pair], sems, i)
    for one in copies:
        one.wait()


def resident_kernel(
    staying, x, inc, rates, sunlit, eddy, span_x, block_inc,
    x_tiles, inc_tiles, x_rows, inc_rows, sems,
):
    load_rows(x, inc, rates, sunlit, eddy, x_tiles, inc_tiles, x_rows, inc_rows, sems)

    def body(t, carry):
        for i in range(8):
            j = t * 8 + i
            q = staying[j]
            span_x[pl.ds(q * ROW, FIELDS), :] = x_rows[pl.ds(j * ROW, FIELDS), :]
            source = jnp.minimum(q, COLS - 1)
            block_inc[pl.ds(j * ROW, ROW), :] = inc_rows[pl.ds(source * ROW, ROW), :]
        return carry

    lax.fori_loop(0, COLS // 8, body, 0)


def tile_block(tiles, g, f):
    return jnp.concatenate(
        [tiles[pl.ds((g * 16 + i) * 48 + f * 8, 8), :] for i in range(16)], axis=0
    )


def row_block(rows, g, f):
    return jnp.concatenate(
        [rows[pl.ds((g * 128 + i * 8) * ROW + f, 8, stride=ROW), :] for i in range(16)], axis=0
    )


def transpose_in(load_x, load_inc, wind, right):
    def body(g, carry):
        for f in range(FIELDS):
            x = load_x(g, f)
            if f in RICHARDSON:
                wind[RICHARDSON[f], pl.ds(g * GROUP, LEV), :] = x.T
            right[f, pl.ds(g * GROUP, LEV), :] = (x + load_inc(g, f)).T
        return carry

    lax.fori_loop(0, 8, body, 0)


def transpose_out(right, tiles, out, sems):
    copies = []
    for g, pair in enumerate(chunked(tiles, out, 8)):
        def body(f, carry):
            block = right[f, pl.ds(g * GROUP, LEV), :].T
            for i in range(16):
                tiles[pl.ds((g * 16 + i) * 48 + f * 8, 8), :] = block[i * 8 : (i + 1) * 8]
            return carry

        lax.fori_loop(0, FIELDS, body, 0, unroll=True)
        copies += copy_chunks([pair], sems, g)
    return copies


def level(ref, f, k):
    return ref[f, pl.ds(k, 8, stride=GROUP), :]


def put_level(ref, f, k, value):
    ref[f, pl.ds(k, 8, stride=GROUP), :] = value


def interface_weight(eddy, upper, lower):
    lapse = upper[0] - lower[0]
    u = upper[1] - lower[1]
    v = upper[2] - lower[2]
    shear = u * u + v * v + 0.1
    unstable = lapse < 0.0
    stable_root = shear + 10.0 * lapse
    top = jnp.where(unstable, shear - 8.0 * lapse, shear * shear)
    bottom = jnp.where(unstable, shear - lapse, stable_root * stable_root)
    wind = eddy * (top / bottom)
    return (1.35 * wind, wind)


def solve(wind, right, factor, forcing, eddy):
    for f in range(FIELDS):
        put_level(right, f, LEV - 1, level(right, f, LEV - 1) + forcing[f])

    def state(k):
        return [level(wind, i, k) for i in range(3)]

    zero = jnp.zeros((8, 128), jnp.float32)

    def eliminate(i, carry):
        excess, moved, above, below = carry
        ks = (i, LEV - 1 - i)
        inner = (state(i + 1), state(LEV - 2 - i))
        weights = (
            interface_weight(eddy, above, inner[0]),
            interface_weight(eddy, inner[1], below),
        )
        new_excess = [[], []]
        new_moved = [[], []]
        for side in range(2):
            ratio = []
            inverse = []
            for m in range(2):
                base = 1.0 + excess[side][m]
                inv = 1.0 / (base + weights[side][m])
                out = weights[side][m] * inv
                factor[side, m, i] = out
                ratio.append(out)
                inverse.append(inv)
                new_excess[side].append(base * out)
            for f in range(FIELDS):
                m = 0 if f in HEAT else 1
                z = level(right, f, ks[side]) + moved[side][f]
                put_level(right, f, ks[side], z * inverse[m])
                new_moved[side].append(z * ratio[m])
        return new_excess, new_moved, inner[0], inner[1]

    start = ([[zero] * 2] * 2, [[zero] * FIELDS] * 2, state(0), state(LEV - 1))
    half = LEV // 2
    excess, moved, above, below = lax.fori_loop(0, half - 1, eliminate, start, unroll=3)
    weight = interface_weight(eddy, above, below)
    solved = [[], []]
    for f in range(FIELDS):
        m = 0 if f in HEAT else 1
        w = weight[m]
        a = 1.0 + excess[0][m]
        b = 1.0 + excess[1][m]
        inv = 1.0 / (a * b + w * (a + b))
        za = level(right, f, half - 1) + moved[0][f]
        zb = level(right, f, half) + moved[1][f]
        ya = ((b + w) * za + w * zb) * inv
        yb = ((a + w) * zb + w * za) * inv
        put_level(right, f, half - 1, ya)
        put_level(right, f, half, yb)
        solved[0].append(ya)
        solved[1].append(yb)

    def substitute(i, carry):
        step = half - 2 - i
        ks = (step, LEV - 1 - step)
        new = [[], []]
        for side in range(2):
            ratio = [factor[side, m, step] for m in range(2)]
            for f in range(FIELDS):
                m = 0 if f in HEAT else 1
                y = level(right, f, ks[side]) + ratio[m] * carry[side][f]
                put_level(right, f, ks[side], y)
                new[side].append(y)
        return new

    lax.fori_loop(0, half - 1, substitute, solved, unroll=3)


def land(recv_copies, place, put):
    step = PEERS // len(recv_copies)

    def body(p, carry):
        for c in range(CAP):
            put(p, c, place[c, p])
        return carry

    for i, one in enumerate(recv_copies):
        one.wait()
        lax.fori_loop(i * step, (i + 1) * step, body, 0)


def start_landing(rows, rows_in, recv, landed, offset, other, tiles, sems):
    size = landed.shape[1]
    parts = 8
    step = PEERS // parts
    first = copy_chunks([(rows_in, rows)], sems, 0)
    arrivals = copy_chunks(
        [
            (recv.at[pl.ds(i * step, step), pl.ds(offset, size), :], landed.at[pl.ds(i * step, step)])
            for i in range(parts)
        ],
        sems, 1,
    )
    last = copy_chunks([(other, tiles)], sems, 1 + parts)
    first[0].wait()
    return arrivals, last[0]


def block_kernel(
    departing, edges, x, rows_in, recv, out, left_rows, right_rows,
    tiles, rows, landed, wind, right, factor, scalars, sems,
):
    arrivals, last = start_landing(rows, rows_in, recv, landed, X_PART, x, tiles, sems)

    def put(p, c, j):
        rows[pl.ds(j * ROW, ROW), :] = landed[p, pl.ds(c * ROW, ROW), :]

    land(arrivals, departing, put)
    last.wait()
    transpose_in(
        lambda g, f: tile_block(tiles, g, f), lambda g, f: row_block(rows, g, f), wind, right
    )
    for g in range(8):
        scalars[0, pl.ds(g * GROUP, LEV), :] = row_block(rows, g, FIELDS).T
    solve(
        wind, right, factor,
        [level(scalars, 0, f) for f in range(FIELDS)],
        level(scalars, 0, FIELDS),
    )
    copies = transpose_out(right, tiles, out, sems)

    def edge(k, carry):
        for side, edge_out in ((0, left_rows), (1, right_rows)):
            j = edges[side, k]
            base = (j >> 3) * 48 + (j & 7)
            edge_out[pl.ds(k * FIELDS, FIELDS), :] = tiles[pl.ds(base, FIELDS, stride=8), :]
        return carry

    lax.fori_loop(0, EDGE, edge, 0, unroll=4)
    for one in copies:
        one.wait()


def span_kernel(
    arriving, inc, rates, sunlit, eddy, rows_in, recv, out,
    tiles, rows, landed, wind, right, factor, sems,
):
    arrivals, last = start_landing(rows, rows_in, recv, landed, 0, inc, tiles, sems)

    def put(p, c, q):
        rows[pl.ds(q * ROW, FIELDS), :] = landed[p, pl.ds(c * FIELDS, FIELDS), :]

    land(arrivals, arriving, put)
    last.wait()
    transpose_in(
        lambda g, f: row_block(rows, g, f), lambda g, f: tile_block(tiles, g, f), wind, right
    )
    lit = 0.5 + sunlit[...].astype(jnp.float32)
    forcing = [
        jnp.concatenate([rates[pl.ds(f, 1), pl.ds(g * 128, 128)] for g in range(8)], axis=0) * lit
        for f in range(FIELDS)
    ]
    solve(wind, right, factor, forcing, eddy[...])
    for one in transpose_out(right, tiles, out, sems):
        one.wait()


def average_kernel(edges, column, own_left, own_right, far_left, far_right, out, buf, sides, sems):
    load = copy_chunks([(column, buf)], sems, 0)
    load += copy_chunks(
        [(one, sides.at[i]) for i, one in enumerate((own_left, own_right, far_left, far_right))],
        sems, 1,
    )
    for one in load:
        one.wait()

    def body(k, carry):
        for side in range(2):
            j = edges[side, k]
            base = (j >> 3) * 48 + (j & 7)
            rows = pl.ds(k * FIELDS, FIELDS)
            buf[pl.ds(base, FIELDS, stride=8), :] = (sides[side, rows, :] + sides[2 + side, rows, :]) * 0.5
        return carry

    lax.fori_loop(0, EDGE, body, 0, unroll=4)
    for one in copy_chunks(chunked(buf, out, 4), sems, 0):
        one.wait()


def shape(*dims):
    return jax.ShapeDtypeStruct(dims, jnp.float32)


def spec(space):
    return pl.BlockSpec(memory_space=space)


def call(kernel, operands, outputs, scratch, sem_count, cost=None):
    return pl.pallas_call(
        kernel,
        out_shape=tuple(one for _, one in outputs),
        in_specs=[spec(space) for space, _ in operands],
        out_specs=tuple(spec(space) for space, _ in outputs),
        scratch_shapes=[
            *(pltpu.VMEM(dims, jnp.float32) for dims in scratch),
            pltpu.SemaphoreType.DMA((sem_count,)),
        ],
        compiler_params=pltpu.CompilerParams(vmem_limit_bytes=VMEM_LIMIT),
        cost_estimate=cost,
    )(*(array for _, array in operands))


def on_device(
    dynamics_profile_values,
    parameterized_increments,
    ground_exchange_rates,
    sunlit_indicator,
    eddy_coefficient_scale,
    departing_profile_indices,
    arriving_parcel_places,
    resident_parcel_place,
    boundary_profile_indices,
):
    smem, vmem, hbm = pltpu.SMEM, pltpu.VMEM, pl.ANY
    departing = (smem, departing_profile_indices[0].T)
    arriving = (smem, arriving_parcel_places[0].T)
    staying = (smem, resident_parcel_place.reshape(-1))
    edges = (smem, boundary_profile_indices[0])
    x = (hbm, to_tiles(dynamics_profile_values))
    inc = (hbm, to_tiles(parameterized_increments))
    physics = (
        (vmem, ground_exchange_rates),
        (vmem, sunlit_indicator.reshape(8, LEV)),
        (vmem, eddy_coefficient_scale.reshape(8, LEV)),
    )
    whole = (COLS * FIELDS, LEV)
    rows = (ROWS_ALLOC, LEV)
    side = (EDGE * FIELDS, LEV)
    transposed = ((3, 8 * GROUP, LEV), (FIELDS, 8 * GROUP, LEV), (2, 2, LEV // 2, 8, LEV))

    (send,) = call(
        pack_kernel, (departing, arriving, x, inc, *physics), ((hbm, shape(PEERS * MESSAGE, LEV)),),
        (whole, whole, rows, rows, (PEERS * MESSAGE, LEV)), 8,
    )
    recv = lax.all_to_all(
        send.reshape(PEERS, MESSAGE, LEV), ("blk", "sub"), split_axis=0, concat_axis=0, tiled=True
    )
    span_rows, block_rows = call(
        resident_kernel, (staying, x, inc, *physics), ((vmem, shape(*rows)), (vmem, shape(*rows))),
        (whole, whole, rows, rows), 8,
        pl.CostEstimate(flops=0, bytes_accessed=14 * 2**20, transcendentals=0),
    )
    column, left_rows, right_rows = call(
        block_kernel, (departing, edges, x, (hbm, block_rows), (hbm, recv)),
        ((hbm, shape(*whole)), (vmem, shape(*side)), (vmem, shape(*side))),
        (whole, rows, (PEERS, CAP * ROW, LEV), *transposed, (1, 8 * GROUP, LEV)), 10,
    )
    count = lax.axis_size("blk")
    far_left = lax.ppermute(right_rows, "blk", [(i, (i + 1) % count) for i in range(count)])
    far_right = lax.ppermute(left_rows, "blk", [((i + 1) % count, i) for i in range(count)])
    (span_out,) = call(
        span_kernel, (arriving, inc, *physics, (hbm, span_rows), (hbm, recv)),
        ((hbm, shape(*whole)),),
        (whole, rows, (PEERS, X_PART, LEV), *transposed), 10,
        pl.CostEstimate(flops=10**9, bytes_accessed=20 * 2**20, transcendentals=0),
    )
    (column,) = call(
        average_kernel,
        (edges, *((hbm, one) for one in (column, left_rows, right_rows, far_left, far_right))),
        ((hbm, shape(*whole)),),
        (whole, (4, *side)), 5,
    )
    return from_tiles(span_out), from_tiles(column)


def solution(mesh):
    one = P(("blk", "sub"))
    placed = (one, one, P(None, ("blk", "sub")), one, one, one, one, one, one)
    return jax.shard_map(
        on_device, mesh=mesh, in_specs=placed, out_specs=(one, one), check_vma=False
    )
```

time: 151 us -> 135 us (0.89)
  the two profiles are of different devices: /device:TPU:0 before, /device:TPU:1 now
where the time goes in v1:
time: 135 us
  waiting for transfers between devices  74.1 us (55%)
  Pallas kernels  45.6 us (34%)
  starting transfers between devices  13.7 us (10%)
    all_to_all x1, waiting for transfers between devices, on_device(): lax.all_to_all(send.reshape(PEERS, MESSAGE, LEV), ('blk', 'sub'), split_a...  74.1 us
    pallas_call x5, Pallas kernels, call(): pl.pallas_call(kernel, out_shape=tuple((one for _, one in outputs)), in_s...  45.6 us
    all_to_all x1, starting transfers between devices, on_device(): lax.all_to_all(send.reshape(PEERS, MESSAGE, LEV), ('blk', 'sub'), split_a...  11.9 us
  transfers between devices with their start and end apart: 3, of which 1 were waited for; matrix products, arithmetic and copies ran while one was open for 0% of the time, Pallas kernels for 15%

profile of v1, /device:TPU:1, one launch (start us, length us, event | category | flops | bytes accessed | tf_op | source)
XLA Modules:
  0.0 134.9 jit_solution(12260154003815755303)
XLA Ops:
  0.6 8.6 %shard_map.105 = f32[13312,128]{1,0:T(8,128)} custom-call(s32[8,128]{1,0:T(8,128)} %bitcast.46, s32[8,128]{1,0:T(8,128)} %bitcast.48, f32[6144,128]{1,0:T(8,128)} %bitcast.34, f32[6144,128]{1,0:T(8,128)} %bitcast.31, f32[6,1024]{1,0:T(8,128)} %rates.5, s32[8,128]{1,0:T(8,128)} %bitcast.40, f32[8,128]{1,0:T(8,128)} %bitcast.43), custom_call_target="tpu_custom_call" | custom-call | tf_op jit(solution)/shard_map/pallas_call | solution.py:377
  9.2 11.9 %all-to-all-start = ((f32[128,104,128]{2,1,0:T(8,128)}), f32[128,104,128]{2,1,0:T(8,128)}, u32[]{:S(2)}, u32[]{:S(2)}) async-start(f32[128,104,128]{2,1,0:T(8,128)} %bitcast.37), calls=%async_computation | async-start | bytes 13631488 | tf_op jit(solution)/shard_map/all_to_all | solution.py:423
  21.1 9.5 %shard_map.104 = (f32[7176,128]{1,0:T(8,128)}, f32[7176,128]{1,0:T(8,128)}) custom-call(s32[1024]{0:T(1024)} %bitcast.52, f32[6144,128]{1,0:T(8,128)} %bitcast.35, f32[6144,128]{1,0:T(8,128)} %bitcast.32, f32[6,1024]{1,0:T(8,128)} %rates.5, s32[8,128]{1,0:T(8,128)} %bitcast.41, f32[8,128]{1,0:T(8,128)} %bitcast.44), custom_call_target="tpu_custom_call" | custom-call | bytes 14680064 | tf_op jit(solution)/shard_map/pallas_call | solution.py:377
  30.6 74.1 %all-to-all-done.recv = f32[128,104,128]{2,1,0:T(8,128)} async-done(((f32[128,104,128]{2,1,0:T(8,128)}), f32[128,104,128]{2,1,0:T(8,128)}, u32[]{:S(2)}, u32[]{:S(2)}) %all-to-all-start) | async-done | bytes 6815776 | tf_op jit(solution)/shard_map/all_to_all | solution.py:423
  104.7 11.6 %shard_map.107 = (f32[6144,128]{1,0:T(8,128)}, f32[768,128]{1,0:T(8,128)}, f32[768,128]{1,0:T(8,128)}) custom-call(s32[8,128]{1,0:T(8,128)} %bitcast.47, s32[2,128]{1,0:T(2,128)} %bitcast.50, f32[6144,128]{1,0:T(8,128)} %bitcast.36, f32[7176,128]{1,0:T(8,128)} %get-tuple-element.8.rows_in, f32[128,104,128]{2,1,0:T(8,128)} %all-to-all-done.recv), custom_call_target="tpu_custom_call" | custom-call | tf_op jit(solution)/shard_map/pallas_call | solution.py:377
  116.2 0.1 collective-permute-start.1
  116.3 1.7 %collective-permute-start = (f32[768,128]{1,0:T(8,128)}, f32[768,128]{1,0:T(8,128)S(1)}, u32[]{:S(2)}, u32[]{:S(2)}) collective-permute-start(f32[768,128]{1,0:T(8,128)} %get-tuple-element.11.own_right), channel_id=1, source_target_pairs={{0,4},{4,8},{8,12},{12,16},{16,20},{20,24},{24,28},{28,32},{32,36}... | collective-permute-start | bytes 1179656 | tf_op jit(solution)/shard_map/ppermute | solution.py:437
  118.1 10.5 %shard_map.106 = f32[6144,128]{1,0:T(8,128)} custom-call(s32[8,128]{1,0:T(8,128)} %bitcast.49, f32[6144,128]{1,0:T(8,128)} %bitcast.33, f32[6,1024]{1,0:T(8,128)} %rates.5, s32[8,128]{1,0:T(8,128)} %bitcast.42, f32[8,128]{1,0:T(8,128)} %bitcast.45, f32[7176,128]{1,0:T(8,128)} %get-tuple-element.7.rows_in, f32[128,104,128]{2,1,0:T(8,128)} %all-to-all-done.recv), custom_call_target="tpu_custom_call" | custom-call | flops 1000000000 | bytes 20971520 | tf_op jit(solution)/shard_map/pallas_call | solution.py:377
  128.6 0.0 collective-permute-done.1.far_right
  128.6 0.0 copy-start
  128.6 0.0 collective-permute-done.far_left
  128.6 0.0 copy-start.1
  128.6 0.7 copy-done
  129.4 0.1 copy-done.1
  129.5 5.5 %shard_map.108 = f32[6144,128]{1,0:T(8,128)} custom-call(s32[2,128]{1,0:T(2,128)} %bitcast.51, f32[6144,128]{1,0:T(8,128)} %get-tuple-element.9.column, f32[768,128]{1,0:T(8,128)} %get-tuple-element.10.own_left, f32[768,128]{1,0:T(8,128)} %get-tuple-element.11.own_right, f32[768,128]{1,0:T(8,128)} %copy-done.1, f32[768,128]{1,0:T(8,128)} %copy-done), custom_call_target="tpu_custom_call" | custom-call | tf_op jit(solution)/shard_map/pallas_call | solution.py:377
Async XLA Ops:
  9.2 95.5 %all-to-all-start = ((f32[128,104,128]{2,1,0:T(8,128)}), f32[128,104,128]{2,1,0:T(8,128)}, u32[]{:S(2)}, u32[]{:S(2)}) async-start(f32[128,104,128]{2,1,0:T(8,128)} %bitcast.37), calls=%async_computation | async-start | bytes 13631488 | tf_op jit(solution)/shard_map/all_to_all | solution.py:423
  116.2 12.4 %collective-permute-start.1 = (f32[768,128]{1,0:T(8,128)}, f32[768,128]{1,0:T(8,128)S(1)}, u32[]{:S(2)}, u32[]{:S(2)}) collective-permute-start(f32[768,128]{1,0:T(8,128)} %get-tuple-element.10.own_left), channel_id=1, source_target_pairs={{4,0},{8,4},{12,8},{16,12},{20,16},{24,20},{28,24},{32,28},{36,32}... | collective-permute-start | bytes 1179656 | tf_op jit(solution)/shard_map/ppermute | solution.py:438
  116.3 12.3 %collective-permute-start = (f32[768,128]{1,0:T(8,128)}, f32[768,128]{1,0:T(8,128)S(1)}, u32[]{:S(2)}, u32[]{:S(2)}) collective-permute-start(f32[768,128]{1,0:T(8,128)} %get-tuple-element.11.own_right), channel_id=1, source_target_pairs={{0,4},{4,8},{8,12},{12,16},{16,20},{20,24},{24,28},{28,32},{32,36}... | collective-permute-start | bytes 1179656 | tf_op jit(solution)/shard_map/ppermute | solution.py:437
  128.6 0.8 copy-start
  128.6 0.9 copy-start.1

commit v2 on v1

--- a/solution.py
+++ b/solution.py
@@ -14,8 +14,17 @@
 ROW = 7
 DUMP = COLS
 ROWS_ALLOC = 7176
-X_PART = CAP * FIELDS
-MESSAGE = X_PART + CAP * ROW
+SLOTS = 11
+SCALARS_AT = SLOTS * FIELDS
+MESSAGE = 72
+HOP = 8
+RESENT = CAP * FIELDS
+SPARE = PEERS * MESSAGE
+PACKED = SPARE + 8
+LANDED = SPARE + 32
+PLAN = 256
+PLAN_COUNT = 128
+PLAN_FAILED = 129
 GROUP = 137
 VMEM_LIMIT = 60 * 2**20
 HEAT = (0, 1, 4, 5)
@@ -79,29 +88,196 @@
             spread_rows(tiles, rows, i * count, count)
 
 
+def device_index():
+    return lax.axis_index("blk") * lax.axis_size("sub") + lax.axis_index("sub")
+
+
+def wrap(index):
+    return index & (PEERS - 1)
+
+
+def fold(offset):
+    return jnp.minimum(offset, PEERS - offset)
+
+
+def fill_tables(departing, arriving, tables, info):
+    out_places = departing[...]
+    in_places = arriving[...]
+    slot = lax.broadcasted_iota(jnp.int32, (CAP, PEERS), 0)
+    peer = lax.broadcasted_iota(jnp.int32, (CAP, PEERS), 1)
+    leaving = jnp.sum((out_places < COLS).astype(jnp.int32), axis=0, keepdims=True)
+    coming = jnp.sum((in_places < COLS).astype(jnp.int32), axis=0, keepdims=True)
+    base = peer * MESSAGE
+    place = coming + slot
+    tables[0:8] = jnp.minimum(out_places, COLS - 1) * ROW
+    tables[8:16] = jnp.where(
+        (slot < leaving) & (place < SLOTS), base + place * FIELDS, SPARE
+    )
+    tables[16:24] = jnp.minimum(in_places, COLS - 1) * ROW
+    tables[24:32] = jnp.where(slot < coming, base + slot * FIELDS, SPARE)
+    counts = jnp.where(slot == 0, leaving, coming)
+    tables[32:40] = counts
+    info[...] = counts
+
+
+def make_plan(me, counts, plan, fill, used):
+    def start(o, carry):
+        p = wrap(me + o)
+        fill[o] = jnp.minimum(counts(0, p) + counts(1, p), SLOTS)
+        used[o] = 0
+        return carry
+
+    lax.fori_loop(1, PEERS // 2, start, 0)
+    for o in (0, PEERS // 2):
+        fill[o] = SLOTS
+        used[o] = 1
+
+    def offset(o, carry):
+        p = wrap(me + o)
+        leaving = counts(0, p)
+        coming = counts(1, p)
+        excess = jnp.maximum(leaving + coming - SLOTS, 0)
+        middle = o == PEERS // 2
+
+        def column(t, carry):
+            last, count, failed = carry
+
+            def search(state):
+                tries, u, _ = state
+                u = jnp.where(u == PEERS - 1, 1, u + 1)
+                taken = (fill[fold(u)] >= SLOTS) | (used[fold(wrap(o - u))] > 0)
+                return tries + 1, u, taken
+
+            tries, u, taken = lax.while_loop(
+                lambda state: state[2] & (state[0] < PEERS), search,
+                (jnp.int32(0), last, jnp.bool_(True)),
+            )
+            found = jnp.logical_not(taken)
+            r = fill[fold(u)]
+            slot = leaving - excess + jnp.where(middle, 2 * t, t)
+            mirror_slot = jnp.where(middle, slot + 1, coming - excess + t)
+            both = jnp.logical_not(middle) | (2 * t + 1 < excess)
+
+            @pl.when(found)
+            def _():
+                fill[fold(u)] = r + 1
+                used[fold(wrap(o - u))] = 1
+                plan[count] = o | (u << 7) | (r << 14) | (slot << 18)
+                plan[count + 1] = (PEERS - o) | ((PEERS - u) << 7) | (r << 14) | (mirror_slot << 18)
+
+            count = count + jnp.where(found, jnp.where(both, 2, 1), 0)
+            return u, count, failed | taken.astype(jnp.int32)
+
+        rounds = jnp.where(middle, (excess + 1) >> 1, excess)
+        return lax.fori_loop(0, rounds, column, carry)
+
+    zero = jnp.int32(0)
+    _, count, failed = lax.fori_loop(1, PEERS // 2 + 1, offset, (zero, zero, zero))
+    plan[PLAN_COUNT] = count
+    plan[PLAN_FAILED] = failed
+
+
+def planned(plan, i):
+    entry = plan[i]
+    o = entry & 127
+    u = (entry >> 7) & 127
+    return o, u, (entry >> 14) & 15, (entry >> 18) & 15
+
+
 def pack_kernel(
-    departing, arriving, x, inc, rates, sunlit, eddy, send,
-    x_tiles, inc_tiles, x_rows, inc_rows, packed, sems,
+    departing, arriving, x, inc, rates, sunlit, eddy, send, plan, info,
+    x_tiles, inc_tiles, x_rows, inc_rows, packed, tables, places, fill, used, sems, table_sem,
 ):
-    load_rows(x, inc, rates, sunlit, eddy, x_tiles, inc_tiles, x_rows, inc_rows, sems)
+    parts = 4
+    x_copies = copy_chunks(chunked(x, x_tiles, parts), sems, 0)
+    inc_copies = copy_chunks(chunked(inc, inc_tiles, parts), sems, parts)
+    fill_tables(departing, arriving, tables, info)
+    move = pltpu.make_async_copy(tables, places, table_sem.at[0])
+    move.start()
+    spread_scalars(rates, sunlit, eddy, inc_rows)
+    move.wait()
+    me = device_index()
+    make_plan(me, lambda row, p: places[32 + row, p], plan, fill, used)
+    count = COLS // 8 // parts
+    for copies, tiles, rows in ((x_copies, x_tiles, x_rows), (inc_copies, inc_tiles, inc_rows)):
+        for i, one in enumerate(copies):
+            one.wait()
+            spread_rows(tiles, rows, i * count, count)
+
+    def relay(i, carry):
+        o, u, r, c = planned(plan, i)
+        source = places[c, wrap(me + o)]
+        target = wrap(me + u) * MESSAGE + r * FIELDS
+        packed[pl.ds(target, FIELDS), :] = x_rows[pl.ds(source, FIELDS), :]
+        return carry
+
+    lax.fori_loop(0, plan[PLAN_COUNT], relay, 0)
+    group = lax.broadcasted_iota(jnp.int32, (1, LEV), 1) >> 3
+
+    def body(p, carry):
+        scalars = jnp.zeros((1, LEV), jnp.float32)
+        for c in range(CAP):
+            packed[pl.ds(places[8 + c, p], FIELDS), :] = x_rows[pl.ds(places[c, p], FIELDS), :]
+            row = places[16 + c, p]
+            packed[pl.ds(places[24 + c, p], FIELDS), :] = inc_rows[pl.ds(row, FIELDS), :]
+            scalars = jnp.where(group == c, inc_rows[pl.ds(row + FIELDS, 1), :], scalars)
+        packed[pl.ds(p * MESSAGE + SCALARS_AT, 1), :] = scalars
+        return carry
+
+    parts = 8
+    step = PEERS // parts
+    size = step * MESSAGE
+    copies = []
+    for i in range(parts):
+        lax.fori_loop(i * step, (i + 1) * step, body, 0)
+        part = pl.ds(i * size, size)
+        copies += copy_chunks([(packed.at[part], send.at[part])], sems, i)
+    for one in copies:
+        one.wait()
+
+
+def relay_kernel(plan, recv, prepared, send, windows, sems):
+    del prepared
+    me = device_index()
+    count = plan[PLAN_COUNT]
+
+    def window(i):
+        o, u, r, _ = planned(plan, i)
+        row = r * FIELDS
+        first = pl.multiple_of((row >> 3) << 3, 8)
+        copy = pltpu.make_async_copy(
+            recv.at[wrap(me - u), pl.ds(first, 16), :], windows.at[i], sems.at[i]
+        )
+        return copy, row - first, wrap(me + o - u)
+
+    def fetch(i, carry):
+        window(i)[0].start()
+        return carry
+
+    def forward(i, carry):
+        copy, at, peer = window(i)
+        copy.wait()
+        send[pl.ds(peer * HOP, FIELDS), :] = windows[i, pl.ds(at, FIELDS), :]
+        return carry
+
+    lax.fori_loop(0, count, fetch, 0)
+    lax.fori_loop(0, count, forward, 0)
+
+
+def resend_kernel(departing, x, send, x_tiles, x_rows, packed, sems):
+    (copy,) = copy_chunks([(x, x_tiles)], sems, 0)
+    copy.wait()
+    spread_rows(x_tiles, x_rows, 0, COLS // 8)
 
     def body(p, carry):
         for c in range(CAP):
             j = jnp.minimum(departing[c, p], COLS - 1)
-            packed[pl.ds(p * MESSAGE + c * FIELDS, FIELDS), :] = x_rows[pl.ds(j * ROW, FIELDS), :]
-        for c in range(CAP):
-            q = jnp.minimum(arriving[c, p], COLS - 1)
-            packed[pl.ds(p * MESSAGE + X_PART + c * ROW, ROW), :] = inc_rows[pl.ds(q * ROW, ROW), :]
-        return carry
-
-    parts = 8
-    step = PEERS // parts
-    copies = []
-    for i, pair in enumerate(chunked(packed, send, parts)):
-        lax.fori_loop(i * step, (i + 1) * step, body, 0)
-        copies += copy_chunks([pair], sems, i)
-    for one in copies:
-        one.wait()
+            packed[pl.ds(p * RESENT + c * FIELDS, FIELDS), :] = x_rows[pl.ds(j * ROW, FIELDS), :]
+        return carry
+
+    lax.fori_loop(0, PEERS, body, 0)
+    (copy,) = copy_chunks([(packed, send)], sems, 0)
+    copy.wait()
 
 
 def resident_kernel(
@@ -254,46 +430,45 @@
     lax.fori_loop(0, half - 1, substitute, solved, unroll=3)
 
 
-def land(recv_copies, place, put):
-    step = PEERS // len(recv_copies)
-
-    def body(p, carry):
-        for c in range(CAP):
-            put(p, c, place[c, p])
-        return carry
-
-    for i, one in enumerate(recv_copies):
-        one.wait()
-        lax.fori_loop(i * step, (i + 1) * step, body, 0)
-
-
-def start_landing(rows, rows_in, recv, landed, offset, other, tiles, sems):
-    size = landed.shape[1]
+def land(copies, put):
+    step = PEERS // len(copies)
+    for i, group in enumerate(copies):
+        for one in group:
+            one.wait()
+        lax.fori_loop(i * step, (i + 1) * step, put, 0)
+
+
+def block_kernel(
+    departing, edges, x, rows_in, recv, out, left_rows, right_rows,
+    tiles, rows, landed, landed_scalars, turned, wind, right, factor, scalars, sems,
+):
     parts = 8
     step = PEERS // parts
-    first = copy_chunks([(rows_in, rows)], sems, 0)
-    arrivals = copy_chunks(
-        [
-            (recv.at[pl.ds(i * step, step), pl.ds(offset, size), :], landed.at[pl.ds(i * step, step)])
-            for i in range(parts)
-        ],
-        sems, 1,
-    )
-    last = copy_chunks([(other, tiles)], sems, 1 + parts)
-    first[0].wait()
-    return arrivals, last[0]
-
-
-def block_kernel(
-    departing, edges, x, rows_in, recv, out, left_rows, right_rows,
-    tiles, rows, landed, wind, right, factor, scalars, sems,
-):
-    arrivals, last = start_landing(rows, rows_in, recv, landed, X_PART, x, tiles, sems)
-
-    def put(p, c, j):
-        rows[pl.ds(j * ROW, ROW), :] = landed[p, pl.ds(c * ROW, ROW), :]
-
-    land(arrivals, departing, put)
+    (first,) = copy_chunks([(rows_in, rows)], sems, 0)
+
+    def part(i, offset, size, target):
+        peers = pl.ds(i * step, step)
+        return recv.at[peers, pl.ds(offset, size), :], target.at[peers]
+
+    head = (SCALARS_AT // 8) * 8
+    (turn,) = copy_chunks([(recv.at[:, pl.ds(head, 8), :], landed_scalars)], sems, 1)
+    arrivals = copy_chunks([part(i, 0, CAP * FIELDS, landed) for i in range(parts)], sems, 2)
+    (last,) = copy_chunks([(x, tiles)], sems, 2 + parts)
+    turn.wait()
+    for i in range(PEERS // 8):
+        lines = landed_scalars[pl.ds(i * 8, 8), SCALARS_AT - head, :]
+        for c in range(CAP):
+            turned[c, pl.ds(i * 8, 8), :] = pltpu.roll(lines, (LEV - 8 * c) % LEV, 1)
+    first.wait()
+
+    def put(p, carry):
+        for c in range(CAP):
+            row = departing[c, p] * ROW
+            rows[pl.ds(row, FIELDS), :] = landed[p, pl.ds(c * FIELDS, FIELDS), :]
+            rows[pl.ds(row + FIELDS, 1), :] = turned[c, pl.ds(p, 1), :]
+        return carry
+
+    land([[one] for one in arrivals], put)
     last.wait()
     transpose_in(
         lambda g, f: tile_block(tiles, g, f), lambda g, f: row_block(rows, g, f), wind, right
@@ -319,17 +494,7 @@
         one.wait()
 
 
-def span_kernel(
-    arriving, inc, rates, sunlit, eddy, rows_in, recv, out,
-    tiles, rows, landed, wind, right, factor, sems,
-):
-    arrivals, last = start_landing(rows, rows_in, recv, landed, 0, inc, tiles, sems)
-
-    def put(p, c, q):
-        rows[pl.ds(q * ROW, FIELDS), :] = landed[p, pl.ds(c * FIELDS, FIELDS), :]
-
-    land(arrivals, arriving, put)
-    last.wait()
+def span_half(tiles, rows, rates, sunlit, eddy, out, wind, right, factor, sems):
     transpose_in(
         lambda g, f: row_block(rows, g, f), lambda g, f: tile_block(tiles, g, f), wind, right
     )
@@ -343,6 +508,59 @@
         one.wait()
 
 
+def span_kernel(
+    arriving, plan, info, inc, rates, sunlit, eddy, rows_in, recv, hop, out,
+    tiles, rows, landed, landed_hop, wind, right, factor, sems,
+):
+    parts = 8
+    size = PEERS // parts * MESSAGE
+    (first,) = copy_chunks([(rows_in, rows)], sems, 0)
+    blocks = [pl.ds(i * size, size) for i in range(parts)]
+    arrivals = copy_chunks([(recv.at[one], landed.at[one]) for one in blocks], sems, 1)
+    relayed, last = copy_chunks([(hop, landed_hop), (inc, tiles)], sems, 1 + parts)
+    first.wait()
+
+    def put(p, carry):
+        ahead = info[0, p]
+        base = p * MESSAGE + ahead * FIELDS
+        for c in range(CAP):
+            q = jnp.where(ahead + c < SLOTS, arriving[c, p], DUMP)
+            rows[pl.ds(q * ROW, FIELDS), :] = landed[pl.ds(base + c * FIELDS, FIELDS), :]
+        return carry
+
+    land([[one] for one in arrivals], put)
+    relayed.wait()
+    me = device_index()
+
+    def put_relayed(i, carry):
+        o, u, _, c = planned(plan, i)
+        q = arriving[c, wrap(me - o)]
+        source = wrap(me - o + u) * HOP
+        rows[pl.ds(q * ROW, FIELDS), :] = landed_hop[pl.ds(source, FIELDS), :]
+        return carry
+
+    lax.fori_loop(0, plan[PLAN_COUNT], put_relayed, 0)
+    last.wait()
+    span_half(tiles, rows, rates, sunlit, eddy, out, wind, right, factor, sems)
+
+
+def resent_span_kernel(
+    arriving, inc, rates, sunlit, eddy, rows_in, recv, out,
+    tiles, rows, landed, wind, right, factor, sems,
+):
+    for one in copy_chunks([(rows_in, rows), (recv, landed), (inc, tiles)], sems, 0):
+        one.wait()
+
+    def put(p, carry):
+        for c in range(CAP):
+            q = arriving[c, p]
+            rows[pl.ds(q * ROW, FIELDS), :] = landed[pl.ds(p * RESENT + c * FIELDS, FIELDS), :]
+        return carry
+
+    lax.fori_loop(0, PEERS, put, 0)
+    span_half(tiles, rows, rates, sunlit, eddy, out, wind, right, factor, sems)
+
+
 def average_kernel(edges, column, own_left, own_right, far_left, far_right, out, buf, sides, sems):
     load = copy_chunks([(column, buf)], sems, 0)
     load += copy_chunks(
@@ -365,15 +583,19 @@
         one.wait()
 
 
-def shape(*dims):
-    return jax.ShapeDtypeStruct(dims, jnp.float32)
+def shape(*dims, dtype=jnp.float32):
+    return jax.ShapeDtypeStruct(dims, dtype)
 
 
 def spec(space):
     return pl.BlockSpec(memory_space=space)
 
 
-def call(kernel, operands, outputs, scratch, sem_count, cost=None):
+def cost(flops, mib):
+    return pl.CostEstimate(flops=flops, bytes_accessed=mib * 2**20, transcendentals=0)
+
+
+def call(kernel, operands, outputs, scratch, sem_count, estimate, more=()):
     return pl.pallas_call(
         kernel,
         out_shape=tuple(one for _, one in outputs),
@@ -381,11 +603,18 @@
         out_specs=tuple(spec(space) for space, _ in outputs),
         scratch_shapes=[
             *(pltpu.VMEM(dims, jnp.float32) for dims in scratch),
+            *more,
             pltpu.SemaphoreType.DMA((sem_count,)),
         ],
         compiler_params=pltpu.CompilerParams(vmem_limit_bytes=VMEM_LIMIT),
-        cost_estimate=cost,
+        cost_estimate=estimate,
     )(*(array for _, array in operands))
+
+
+def exchange(rows, sublanes):
+    return lax.all_to_all(
+        rows.reshape(PEERS, sublanes, LEV), ("blk", "sub"), split_axis=0, concat_axis=0, tiled=True
+    )
 
 
 def on_device(
@@ -416,37 +645,76 @@
     side = (EDGE * FIELDS, LEV)
     transposed = ((3, 8 * GROUP, LEV), (FIELDS, 8 * GROUP, LEV), (2, 2, LEV // 2, 8, LEV))
 
-    (send,) = call(
-        pack_kernel, (departing, arriving, x, inc, *physics), ((hbm, shape(PEERS * MESSAGE, LEV)),),
-        (whole, whole, rows, rows, (PEERS * MESSAGE, LEV)), 8,
-    )
-    recv = lax.all_to_all(
-        send.reshape(PEERS, MESSAGE, LEV), ("blk", "sub"), split_axis=0, concat_axis=0, tiled=True
-    )
+    integers = pltpu.VMEM((40, PEERS), jnp.int32)
+
+    send, plan, info = call(
+        pack_kernel, ((vmem, departing[1]), (vmem, arriving[1]), x, inc, *physics),
+        (
+            (hbm, shape(SPARE, LEV)),
+            (smem, shape(PLAN, dtype=jnp.int32)),
+            (vmem, shape(CAP, PEERS, dtype=jnp.int32)),
+        ),
+        (whole, whole, rows, rows, (PACKED, LEV)), 1, cost(0, 14),
+        (
+            integers,
+            pltpu.SMEM((40, PEERS), jnp.int32),
+            pltpu.SMEM((PEERS,), jnp.int32),
+            pltpu.SMEM((PEERS,), jnp.int32),
+            pltpu.SemaphoreType.DMA((8,)),
+        ),
+    )
+    plan = (smem, plan)
+    recv = exchange(send, MESSAGE)
     span_rows, block_rows = call(
         resident_kernel, (staying, x, inc, *physics), ((vmem, shape(*rows)), (vmem, shape(*rows))),
-        (whole, whole, rows, rows), 8,
-        pl.CostEstimate(flops=0, bytes_accessed=14 * 2**20, transcendentals=0),
-    )
+        (whole, whole, rows, rows), 8, cost(0, 14),
+    )
+    (hop,) = call(
+        relay_kernel, (plan, (hbm, recv), (hbm, block_rows)), ((vmem, shape(PEERS * HOP, LEV)),),
+        ((PEERS, 16, LEV),), PEERS, cost(0, 2),
+    )
+    hop = exchange(hop, HOP)
     column, left_rows, right_rows = call(
         block_kernel, (departing, edges, x, (hbm, block_rows), (hbm, recv)),
         ((hbm, shape(*whole)), (vmem, shape(*side)), (vmem, shape(*side))),
-        (whole, rows, (PEERS, CAP * ROW, LEV), *transposed, (1, 8 * GROUP, LEV)), 10,
+        (
+            whole, rows, (PEERS, CAP * FIELDS, LEV), (PEERS, 8, LEV), (CAP, PEERS, LEV),
+            *transposed, (1, 8 * GROUP, LEV),
+        ),
+        11, cost(10**9, 20),
     )
     count = lax.axis_size("blk")
     far_left = lax.ppermute(right_rows, "blk", [(i, (i + 1) % count) for i in range(count)])
     far_right = lax.ppermute(left_rows, "blk", [((i + 1) % count, i) for i in range(count)])
-    (span_out,) = call(
-        span_kernel, (arriving, inc, *physics, (hbm, span_rows), (hbm, recv)),
-        ((hbm, shape(*whole)),),
-        (whole, rows, (PEERS, X_PART, LEV), *transposed), 10,
-        pl.CostEstimate(flops=10**9, bytes_accessed=20 * 2**20, transcendentals=0),
-    )
+
+    def relayed():
+        return call(
+            span_kernel,
+            (
+                arriving, plan, (smem, info), inc, *physics, (hbm, span_rows),
+                (hbm, recv.reshape(SPARE, LEV)), (hbm, hop.reshape(PEERS * HOP, LEV)),
+            ),
+            ((hbm, shape(*whole)),),
+            (whole, rows, (LANDED, LEV), (PEERS * HOP, LEV), *transposed), 11, cost(10**9, 20),
+        )[0]
+
+    def resent():
+        sent = (PEERS * RESENT, LEV)
+        (again,) = call(
+            resend_kernel, (departing, x), ((hbm, shape(*sent)),), (whole, rows, sent), 1, cost(0, 8)
+        )
+        again = exchange(again, RESENT).reshape(sent)
+        return call(
+            resent_span_kernel, (arriving, inc, *physics, (hbm, span_rows), (hbm, again)),
+            ((hbm, shape(*whole)),), (whole, rows, sent, *transposed), 8, cost(10**9, 20),
+        )[0]
+
+    span_out = lax.cond(plan[1][PLAN_FAILED] > 0, resent, relayed)
     (column,) = call(
         average_kernel,
         (edges, *((hbm, one) for one in (column, left_rows, right_rows, far_left, far_right))),
         ((hbm, shape(*whole)),),
-        (whole, (4, *side)), 5,
+        (whole, (4, *side)), 5, cost(0, 8),
     )
     return from_tiles(span_out), from_tiles(column)
 

time: 135 us -> 140 us (1.037)
  the two profiles are of different devices: /device:TPU:1 before, /device:TPU:0 now
where the time goes in v2:
time: 140 us; the launch traced here: 141 us
  waiting for transfers between devices  59.2 us (42%)
  Pallas kernels  57.2 us (41%)
  starting transfers between devices  22.3 us (16%)
  between operations  1.43 us (1%)
    pallas_call x6, Pallas kernels, call(): pl.pallas_call(kernel, out_shape=tuple((one for _, one in outputs)), in_s...  57.2 us
    all_to_all x2, waiting for transfers between devices, exchange(): lax.all_to_all(rows.reshape(PEERS, sublanes, LEV), ('blk', 'sub'), split_...  49.6 us
    all_to_all x2, starting transfers between devices, exchange(): lax.all_to_all(rows.reshape(PEERS, sublanes, LEV), ('blk', 'sub'), split_...  17.4 us
    ppermute x1, waiting for transfers between devices, on_device(): lax.ppermute(right_rows, 'blk', [(i, (i + 1) % count) for i in range(coun...  5.22 us
    ppermute x1, starting transfers between devices, on_device(): lax.ppermute(left_rows, 'blk', [((i + 1) % count, i) for i in range(count)])  4.86 us
    ppermute x1, waiting for transfers between devices, on_device(): lax.ppermute(left_rows, 'blk', [((i + 1) % count, i) for i in range(count)])  4.37 us
  transfers between devices with their start and end apart: 4, of which 3 were waited for; matrix products, arithmetic and copies ran while one was open for 0% of the time, Pallas kernels for 19%

profile of v2, /device:TPU:0, one launch (start us, length us, event | category | flops | bytes accessed | tf_op | source)
XLA Modules:
  0.0 140.7 jit_solution(7136357207792378819)
XLA Ops:
  0.6 14.3 %shard_map.104 = (f32[9216,128]{1,0:T(8,128)}, s32[256]{0:T(256)S(1)}, s32[8,128]{1,0:T(8,128)S(1)}) custom-call(s32[8,128]{1,0:T(8,128)} %bitcast.62, s32[8,128]{1,0:T(8,128)} %bitcast.59, f32[6144,128]{1,0:T(8,128)} %bitcast.41, f32[6144,128]{1,0:T(8,128)} %bitcast.37, f32[6,1024]{1,0:T(8,128)} %rates.3, s32[8,128]{1,0:T(8,128)} %bitcast.51, f32[8,128]{1,0:T(8,128)} %bitcast.55), custom_call_target="tpu_custom_call" | custom-call | bytes 14680064 | tf_op jit(solution)/shard_map/pallas_call | solution.py:599
  14.9 0.0 copy-start
  15.0 0.0 copy-start.1
  15.0 0.0 copy-start.3
  15.0 0.0 copy-start.4
  15.0 11.6 %all-to-all-start.1 = ((f32[128,72,128]{2,1,0:T(8,128)}), f32[128,72,128]{2,1,0:T(8,128)}, u32[]{:S(2)}, u32[]{:S(2)}) async-start(f32[128,72,128]{2,1,0:T(8,128)} %bitcast.47), calls=%async_computation.1 | async-start | bytes 9437184 | tf_op jit(solution)/shard_map/all_to_all | solution.py:615
  26.6 0.0 copy-done
  26.7 0.0 copy-done.1
  26.7 0.0 copy-done.3
  26.7 0.0 copy-done.4
  26.7 8.8 %shard_map.105 = (f32[7176,128]{1,0:T(8,128)}, f32[7176,128]{1,0:T(8,128)}) custom-call(s32[1024]{0:T(1024)} %bitcast.65, f32[6144,128]{1,0:T(8,128)} %bitcast.42, f32[6144,128]{1,0:T(8,128)S(1)} %bitcast.38, f32[6,1024]{1,0:T(8,128)S(1)} %copy-done.1, s32[8,128]{1,0:T(8,128)S(1)} %bitcast.52, f32[8,128]{1,0:T(8,128)S(1)} %bitcast.56), custom_call_target="tpu_custom_call" | custom-call | bytes 14680064 | tf_op jit(solution)/shard_map/pallas_call | solution.py:599
  35.5 49.6 %all-to-all-done.1.recv = f32[128,72,128]{2,1,0:T(8,128)} async-done(((f32[128,72,128]{2,1,0:T(8,128)}), f32[128,72,128]{2,1,0:T(8,128)}, u32[]{:S(2)}, u32[]{:S(2)}) %all-to-all-start.1) | async-done | bytes 4718624 | tf_op jit(solution)/shard_map/all_to_all | solution.py:615
  85.0 0.0 copy-start.6
  85.0 4.4 %shard_map.106 = f32[1024,128]{1,0:T(8,128)} custom-call(s32[256]{0:T(256)S(1)} %get-tuple-element.67.plan, f32[128,72,128]{2,1,0:T(8,128)} %all-to-all-done.1.recv, f32[7176,128]{1,0:T(8,128)} %get-tuple-element.69.prepared.rows_in), custom_call_target="tpu_custom_call" | custom-call | bytes 2097152 | tf_op jit(solution)/shard_map/pallas_call | solution.py:599
  89.4 5.8 %all-to-all-start.2 = ((f32[128,8,128]{2,1,0:T(8,128)}), f32[128,8,128]{2,1,0:T(8,128)}, u32[]{:S(2)}, u32[]{:S(2)}) async-start(f32[128,8,128]{2,1,0:T(8,128)} %bitcast.50), calls=%async_computation.2 | async-start | bytes 1048576 | tf_op jit(solution)/shard_map/all_to_all | solution.py:615
  95.2 0.0 copy-done.6
  95.2 11.8 %shard_map.107 = (f32[6144,128]{1,0:T(8,128)}, f32[768,128]{1,0:T(8,128)}, f32[768,128]{1,0:T(8,128)}) custom-call(s32[8,128]{1,0:T(8,128)S(1)} %bitcast.63, s32[2,128]{1,0:T(2,128)} %bitcast.66, f32[6144,128]{1,0:T(8,128)} %bitcast.43, f32[7176,128]{1,0:T(8,128)} %get-tuple-element.69.prepared.rows_in, f32[128,72,128]{2,1,0:T(8,128)} %all-to-all-done.1.recv), custom_call_target="tpu_custom_call" | custom-call | flops 1000000000 | bytes 20971520 | tf_op jit(solution)/shard_map/pallas_call | solution.py:599
  107.0 4.9 %collective-permute-start.1 = (f32[768,128]{1,0:T(8,128)}, f32[768,128]{1,0:T(8,128)S(1)}, u32[]{:S(2)}, u32[]{:S(2)}) collective-permute-start(f32[768,128]{1,0:T(8,128)} %get-tuple-element.73.own_left), channel_id=1, source_target_pairs={{4,0},{8,4},{12,8},{16,12},{20,16},{24,20},{28,24},{32,28},{36,32}... | collective-permute-start | bytes 1179656 | tf_op jit(solution)/shard_map/ppermute | solution.py:688
  111.8 0.0 collective-permute-start
  111.8 0.6 slice.3
  113.1 4.4 %collective-permute-done.1.far_right = f32[768,128]{1,0:T(8,128)S(1)} collective-permute-done((f32[768,128]{1,0:T(8,128)}, f32[768,128]{1,0:T(8,128)S(1)}, u32[]{:S(2)}, u32[]{:S(2)}) %collective-permute-start.1) | collective-permute-done | bytes 393248 | tf_op jit(solution)/shard_map/ppermute | solution.py:688
  117.5 0.0 copy-start.2
  117.5 5.2 %collective-permute-done.far_left = f32[768,128]{1,0:T(8,128)} collective-permute-done((f32[768,128]{1,0:T(8,128)}, f32[768,128]{1,0:T(8,128)}, u32[]{:S(2)}, u32[]{:S(2)}) %collective-permute-start) | collective-permute-done | bytes 393248 | tf_op jit(solution)/shard_map/ppermute | solution.py:687
  122.7 0.0 copy-done.2
  122.7 0.0 copy-start.5
  122.7 5.6 %shard_map.108 = f32[6144,128]{1,0:T(8,128)} custom-call(s32[2,128]{1,0:T(2,128)} %bitcast.67, f32[6144,128]{1,0:T(8,128)} %get-tuple-element.72.column, f32[768,128]{1,0:T(8,128)} %get-tuple-element.73.own_left, f32[768,128]{1,0:T(8,128)} %get-tuple-element.74.own_right, f32[768,128]{1,0:T(8,128)} %collective-permute-done.far_left, f32[768,128]{1,0:T(8,128)} %copy-done.2), custom_call_target="tpu_custom_call" | custom-call | bytes 8388608 | tf_op jit(solution)/shard_map/pallas_call | solution.py:599
  128.3 0.0 all-to-all-done.2
  128.3 0.0 copy-done.5
  128.3 12.4 %conditional.1 = (f32[6144,128]{1,0:T(8,128)}) conditional(s32[]{:T(128)} %bitcast.16, (f32[128,72,128]{2,1,0:T(8,128)}, f32[128,8,128]{2,1,0:T(8,128)}, s32[8,128]{1,0:T(8,128)S(1)}, s32[256]{0:T(256)S(1)}, s32[8,128]{1,0:T(8,128)S(1)}, /*index=5*/f32[6144,128]{1,0:T(8,128)S(1)}, f32[6,1024]{1,0:T(8,128)S(1)}, s32[8,128]{1,0:T(8,128)S(1)}, ...), branch_computations={%region_0.0_spmd, %region_1.0_spmd} | conditional | flops 1000000000 | bytes 35651592 | solution.py:712
  128.3 12.3 %branch_0_fun.1 = f32[6144,128]{1,0:T(8,128)} custom-call(s32[8,128]{1,0:T(8,128)S(1)} %get-tuple-element.27.arriving, s32[256]{0:T(256)S(1)} %get-tuple-element.40.plan, s32[8,128]{1,0:T(8,128)S(1)} %get-tuple-element.41.info, f32[6144,128]{1,0:T(8,128)S(1)} %get-tuple-element.42.inc, f32[6,1024]{1,0:T(8,128)S(1)} %get-tuple-element.43.rates, ...), custom_call_target="tpu_custom_call" | custom-call | flops 1000000000 | bytes 20971520 | tf_op jit(solution)/shard_map/cond/branch_0_fun/pallas_call | solution.py:599
Async XLA Ops:
  14.9 11.7 %copy-start = (f32[1024,768]{1,0:T(8,128)S(1)}, f32[1024,768]{1,0:T(8,128)}, u32[]{:S(2)}) copy-start(f32[1024,768]{1,0:T(8,128)} %param.12) | copy-start | bytes 9437188
  15.0 11.7 %copy-start.1 = (f32[6,1024]{1,0:T(8,128)S(1)}, f32[6,1024]{1,0:T(8,128)}, u32[]{:S(2)}) copy-start(f32[6,1024]{1,0:T(8,128)} %rates.3) | copy-start | bytes 73732
  15.0 11.7 %copy-start.3 = (s32[1024]{0:T(1024)S(1)}, s32[1024]{0:T(1024)}, u32[]{:S(2)}) copy-start(s32[1024]{0:T(1024)} %param.14) | copy-start | bytes 12292
  15.0 11.7 %copy-start.4 = (f32[1024]{0:T(1024)S(1)}, f32[1024]{0:T(1024)}, u32[]{:S(2)}) copy-start(f32[1024]{0:T(1024)} %param.15) | copy-start | bytes 12292
  15.0 70.0 %all-to-all-start.1 = ((f32[128,72,128]{2,1,0:T(8,128)}), f32[128,72,128]{2,1,0:T(8,128)}, u32[]{:S(2)}, u32[]{:S(2)}) async-start(f32[128,72,128]{2,1,0:T(8,128)} %bitcast.47), calls=%async_computation.1 | async-start | bytes 9437184 | tf_op jit(solution)/shard_map/all_to_all | solution.py:615
  85.0 10.2 %copy-start.6 = (s32[1,128,8]{1,2,0:T(8,128)S(1)}, s32[1,128,8]{1,2,0:T(8,128)}, u32[]{:S(2)}) copy-start(s32[1,128,8]{1,2,0:T(8,128)} %param.16) | copy-start | bytes 12292
  89.4 38.9 %all-to-all-start.2 = ((f32[128,8,128]{2,1,0:T(8,128)}), f32[128,8,128]{2,1,0:T(8,128)}, u32[]{:S(2)}, u32[]{:S(2)}) async-start(f32[128,8,128]{2,1,0:T(8,128)} %bitcast.50), calls=%async_computation.2 | async-start | bytes 1048576 | tf_op jit(solution)/shard_map/all_to_all | solution.py:615
  107.0 10.5 %collective-permute-start.1 = (f32[768,128]{1,0:T(8,128)}, f32[768,128]{1,0:T(8,128)S(1)}, u32[]{:S(2)}, u32[]{:S(2)}) collective-permute-start(f32[768,128]{1,0:T(8,128)} %get-tuple-element.73.own_left), channel_id=1, source_target_pairs={{4,0},{8,4},{12,8},{16,12},{20,16},{24,20},{28,24},{32,28},{36,32}... | collective-permute-start | bytes 1179656 | tf_op jit(solution)/shard_map/ppermute | solution.py:688
  111.8 10.8 %collective-permute-start = (f32[768,128]{1,0:T(8,128)}, f32[768,128]{1,0:T(8,128)}, u32[]{:S(2)}, u32[]{:S(2)}) collective-permute-start(f32[768,128]{1,0:T(8,128)} %get-tuple-element.74.own_right), channel_id=1, source_target_pairs={{0,4},{4,8},{8,12},{12,16},{16,20},{20,24},{24,28},{28,32},{32,36}... | collective-permute-start | bytes 1179656 | tf_op jit(solution)/shard_map/ppermute | solution.py:687
  117.5 5.2 %copy-start.2 = (f32[768,128]{1,0:T(8,128)}, f32[768,128]{1,0:T(8,128)S(1)}, u32[]{:S(2)}) copy-start(f32[768,128]{1,0:T(8,128)S(1)} %collective-permute-done.1.far_right) | copy-start | bytes 1179652
  122.7 5.6 %copy-start.5 = (s32[1,128,8]{1,2,0:T(8,128)S(1)}, s32[1,128,8]{1,2,0:T(8,128)}, u32[]{:S(2)}) copy-start(s32[1,128,8]{1,2,0:T(8,128)} %param.17) | copy-start | bytes 12292

commit v3 on v2

--- a/solution.py
+++ b/solution.py
@@ -15,6 +15,8 @@
 DUMP = COLS
 ROWS_ALLOC = 7176
 SLOTS = 11
+RELAYS = 2
+FACTS, ROOM, USED = 0, 1, 2
 SCALARS_AT = SLOTS * FIELDS
 MESSAGE = 72
 HOP = 8
@@ -26,7 +28,7 @@
 PLAN_COUNT = 128
 PLAN_FAILED = 129
 GROUP = 137
-VMEM_LIMIT = 60 * 2**20
+VMEM_LIMIT = 52 * 2**20
 HEAT = (0, 1, 4, 5)
 RICHARDSON = {0: 0, 2: 1, 3: 2}
 
@@ -96,11 +98,7 @@
     return index & (PEERS - 1)
 
 
-def fold(offset):
-    return jnp.minimum(offset, PEERS - offset)
-
-
-def fill_tables(departing, arriving, tables, info):
+def fill_tables(me, departing, arriving, tables, info):
     out_places = departing[...]
     in_places = arriving[...]
     slot = lax.broadcasted_iota(jnp.int32, (CAP, PEERS), 0)
@@ -115,28 +113,27 @@
     )
     tables[16:24] = jnp.minimum(in_places, COLS - 1) * ROW
     tables[24:32] = jnp.where(slot < coming, base + slot * FIELDS, SPARE)
-    counts = jnp.where(slot == 0, leaving, coming)
-    tables[32:40] = counts
-    info[...] = counts
-
-
-def make_plan(me, counts, plan, fill, used):
-    def start(o, carry):
-        p = wrap(me + o)
-        fill[o] = jnp.minimum(counts(0, p) + counts(1, p), SLOTS)
-        used[o] = 0
-        return carry
-
-    lax.fori_loop(1, PEERS // 2, start, 0)
-    for o in (0, PEERS // 2):
-        fill[o] = SLOTS
-        used[o] = 1
+    info[...] = jnp.where(slot == 0, leaving, coming)
+    leaving, coming = (pltpu.roll(one, PEERS - me, 1) for one in (info[0:1], info[1:2]))
+    total = leaving + coming
+    blocked = wrap(peer) * 2 % PEERS == 0
+    excess = jnp.maximum(total - SLOTS, 0)
+    room = jnp.minimum(jnp.maximum(SLOTS - total, 0), RELAYS)
+    tables[32:40] = jnp.where(
+        slot == FACTS,
+        leaving | (coming << 4) | (excess << 8),
+        jnp.where(slot == ROOM, jnp.where(blocked, 0, room), blocked.astype(jnp.int32)),
+    )
+
+
+def make_plan(table, plan):
+    facts, room, used = (table.at[32 + i] for i in (FACTS, ROOM, USED))
 
     def offset(o, carry):
-        p = wrap(me + o)
-        leaving = counts(0, p)
-        coming = counts(1, p)
-        excess = jnp.maximum(leaving + coming - SLOTS, 0)
+        fact = facts[o]
+        leaving = fact & 15
+        coming = (fact >> 4) & 15
+        excess = fact >> 8
         middle = o == PEERS // 2
 
         def column(t, carry):
@@ -144,24 +141,26 @@
 
             def search(state):
                 tries, u, _ = state
-                u = jnp.where(u == PEERS - 1, 1, u + 1)
-                taken = (fill[fold(u)] >= SLOTS) | (used[fold(wrap(o - u))] > 0)
-                return tries + 1, u, taken
-
-            tries, u, taken = lax.while_loop(
+                u = wrap(u + 1)
+                return tries + 1, u, (room[u] == 0) | (used[wrap(o - u)] > 0)
+
+            _, u, taken = lax.while_loop(
                 lambda state: state[2] & (state[0] < PEERS), search,
                 (jnp.int32(0), last, jnp.bool_(True)),
             )
             found = jnp.logical_not(taken)
-            r = fill[fold(u)]
             slot = leaving - excess + jnp.where(middle, 2 * t, t)
             mirror_slot = jnp.where(middle, slot + 1, coming - excess + t)
             both = jnp.logical_not(middle) | (2 * t + 1 < excess)
 
             @pl.when(found)
             def _():
-                fill[fold(u)] = r + 1
-                used[fold(wrap(o - u))] = 1
+                free = room[u]
+                r = SLOTS - free
+                room[u] = free - 1
+                room[PEERS - u] = free - 1
+                used[wrap(o - u)] = 1
+                used[wrap(u - o)] = 1
                 plan[count] = o | (u << 7) | (r << 14) | (slot << 18)
                 plan[count + 1] = (PEERS - o) | ((PEERS - u) << 7) | (r << 14) | (mirror_slot << 18)
 
@@ -186,18 +185,18 @@
 
 def pack_kernel(
     departing, arriving, x, inc, rates, sunlit, eddy, send, plan, info,
-    x_tiles, inc_tiles, x_rows, inc_rows, packed, tables, places, fill, used, sems, table_sem,
+    x_tiles, inc_tiles, x_rows, inc_rows, packed, tables, places, sems, table_sem,
 ):
     parts = 4
     x_copies = copy_chunks(chunked(x, x_tiles, parts), sems, 0)
     inc_copies = copy_chunks(chunked(inc, inc_tiles, parts), sems, parts)
-    fill_tables(departing, arriving, tables, info)
+    me = device_index()
+    fill_tables(me, departing, arriving, tables, info)
     move = pltpu.make_async_copy(tables, places, table_sem.at[0])
     move.start()
     spread_scalars(rates, sunlit, eddy, inc_rows)
     move.wait()
-    me = device_index()
-    make_plan(me, lambda row, p: places[32 + row, p], plan, fill, used)
+    make_plan(places, plan)
     count = COLS // 8 // parts
     for copies, tiles, rows in ((x_copies, x_tiles, x_rows), (inc_copies, inc_tiles, inc_rows)):
         for i, one in enumerate(copies):
@@ -236,32 +235,20 @@
         one.wait()
 
 
-def relay_kernel(plan, recv, prepared, send, windows, sems):
+def relay_kernel(plan, recv, prepared, send, landed, sems):
     del prepared
     me = device_index()
-    count = plan[PLAN_COUNT]
-
-    def window(i):
+    first = (SLOTS - RELAYS) * FIELDS // 8 * 8
+    (copy,) = copy_chunks([(recv.at[:, pl.ds(first, MESSAGE - first), :], landed)], sems, 0)
+    copy.wait()
+
+    def forward(i, carry):
         o, u, r, _ = planned(plan, i)
-        row = r * FIELDS
-        first = pl.multiple_of((row >> 3) << 3, 8)
-        copy = pltpu.make_async_copy(
-            recv.at[wrap(me - u), pl.ds(first, 16), :], windows.at[i], sems.at[i]
-        )
-        return copy, row - first, wrap(me + o - u)
-
-    def fetch(i, carry):
-        window(i)[0].start()
-        return carry
-
-    def forward(i, carry):
-        copy, at, peer = window(i)
-        copy.wait()
-        send[pl.ds(peer * HOP, FIELDS), :] = windows[i, pl.ds(at, FIELDS), :]
-        return carry
-
-    lax.fori_loop(0, count, fetch, 0)
-    lax.fori_loop(0, count, forward, 0)
+        row = landed[wrap(me - u), pl.ds(r * FIELDS - first, FIELDS), :]
+        send[pl.ds(wrap(me + o - u) * HOP, FIELDS), :] = row
+        return carry
+
+    lax.fori_loop(0, plan[PLAN_COUNT], forward, 0)
 
 
 def resend_kernel(departing, x, send, x_tiles, x_rows, packed, sems):
@@ -561,24 +548,29 @@
     span_half(tiles, rows, rates, sunlit, eddy, out, wind, right, factor, sems)
 
 
-def average_kernel(edges, column, own_left, own_right, far_left, far_right, out, buf, sides, sems):
-    load = copy_chunks([(column, buf)], sems, 0)
-    load += copy_chunks(
-        [(one, sides.at[i]) for i, one in enumerate((own_left, own_right, far_left, far_right))],
+def average_kernel(
+    edges, column, own_left, own_right, far_left, far_right, after, out, buf, sides, sems
+):
+    del after
+    load = copy_chunks(
+        [(one, sides.at[i]) for i, one in enumerate((own_left, far_left, own_right, far_right))],
         sems, 1,
     )
-    for one in load:
+    load += copy_chunks([(column, buf)], sems, 0)
+    for one in load[:4]:
         one.wait()
+    for side in range(2):
+        sides[2 * side] = (sides[2 * side] + sides[2 * side + 1]) * 0.5
+    load[4].wait()
 
     def body(k, carry):
         for side in range(2):
             j = edges[side, k]
             base = (j >> 3) * 48 + (j & 7)
-            rows = pl.ds(k * FIELDS, FIELDS)
-            buf[pl.ds(base, FIELDS, stride=8), :] = (sides[side, rows, :] + sides[2 + side, rows, :]) * 0.5
-        return carry
-
-    lax.fori_loop(0, EDGE, body, 0, unroll=4)
+            buf[pl.ds(base, FIELDS, stride=8), :] = sides[2 * side, pl.ds(k * FIELDS, FIELDS), :]
+        return carry
+
+    lax.fori_loop(0, EDGE, body, 0, unroll=8)
     for one in copy_chunks(chunked(buf, out, 4), sems, 0):
         one.wait()
 
@@ -658,8 +650,6 @@
         (
             integers,
             pltpu.SMEM((40, PEERS), jnp.int32),
-            pltpu.SMEM((PEERS,), jnp.int32),
-            pltpu.SMEM((PEERS,), jnp.int32),
             pltpu.SemaphoreType.DMA((8,)),
         ),
     )
@@ -671,7 +661,7 @@
     )
     (hop,) = call(
         relay_kernel, (plan, (hbm, recv), (hbm, block_rows)), ((vmem, shape(PEERS * HOP, LEV)),),
-        ((PEERS, 16, LEV),), PEERS, cost(0, 2),
+        ((PEERS, MESSAGE - (SLOTS - RELAYS) * FIELDS // 8 * 8, LEV),), 1, cost(0, 2),
     )
     hop = exchange(hop, HOP)
     column, left_rows, right_rows = call(
@@ -712,7 +702,7 @@
     span_out = lax.cond(plan[1][PLAN_FAILED] > 0, resent, relayed)
     (column,) = call(
         average_kernel,
-        (edges, *((hbm, one) for one in (column, left_rows, right_rows, far_left, far_right))),
+        (edges, *((hbm, one) for one in (column, left_rows, right_rows, far_left, far_right, span_out))),
         ((hbm, shape(*whole)),),
         (whole, (4, *side)), 5, cost(0, 8),
     )

time: 140 us -> 127 us (0.907); the launches traced: 141 us -> 125 us
  waiting for transfers between devices: 59.2 us -> 49.1 us
  Pallas kernels: 57.2 us -> 53 us
    ppermute x1, waiting for transfers between devices: 5.22 us -> 0.01 us  [on_device(): lax.ppermute(right_rows, 'blk', [(i, (i + 1) % count) for i in range(coun...]
    ppermute x1, waiting for transfers between devices: 4.37 us -> 0.01 us  [on_device(): lax.ppermute(left_rows, 'blk', [((i + 1) % count, i) for i in range(count)])]
    pallas_call x6, Pallas kernels: 57.2 us -> 53 us  [call(): pl.pallas_call(kernel, out_shape=tuple((one for _, one in outputs)), in_s...]
  transfers between devices with their start and end apart: 4 -> 4, of which waited for: 3 -> 1; matrix products, arithmetic and copies ran while one was open for 0% -> 0% of each run, Pallas kernels for 19% -> 25%
where the time goes in v3:
time: 127 us; the launch traced here: 125 us
  Pallas kernels  53 us (42%)
  waiting for transfers between devices  49.1 us (39%)
  starting transfers between devices  21.2 us (17%)
  between operations  1.46 us (1%)
    pallas_call x6, Pallas kernels, call(): pl.pallas_call(kernel, out_shape=tuple((one for _, one in outputs)), in_s...  53 us
    all_to_all x2, waiting for transfers between devices, exchange(): lax.all_to_all(rows.reshape(PEERS, sublanes, LEV), ('blk', 'sub'), split_...  49.1 us
    all_to_all x2, starting transfers between devices, exchange(): lax.all_to_all(rows.reshape(PEERS, sublanes, LEV), ('blk', 'sub'), split_...  16.3 us
    ppermute x1, starting transfers between devices, on_device(): lax.ppermute(left_rows, 'blk', [((i + 1) % count, i) for i in range(count)])  4.94 us
  transfers between devices with their start and end apart: 4, of which 1 were waited for; matrix products, arithmetic and copies ran while one was open for 0% of the time, Pallas kernels for 25%

profile of v3, /device:TPU:0, one launch (start us, length us, event | category | flops | bytes accessed | tf_op | source)
XLA Modules:
  0.0 125.4 jit_solution(10279435760412955194)
XLA Ops:
  0.6 12.3 %shard_map.104 = (f32[9216,128]{1,0:T(8,128)}, s32[256]{0:T(256)S(1)}, s32[8,128]{1,0:T(8,128)S(1)}) custom-call(s32[8,128]{1,0:T(8,128)} %bitcast.65, s32[8,128]{1,0:T(8,128)} %bitcast.62, f32[6144,128]{1,0:T(8,128)} %bitcast.44, f32[6144,128]{1,0:T(8,128)} %bitcast.40, f32[6,1024]{1,0:T(8,128)} %rates.3, s32[8,128]{1,0:T(8,128)} %bitcast.54, f32[8,128]{1,0:T(8,128)} %bitcast.58), custom_call_target="tpu_custom_call" | custom-call | bytes 14680064 | tf_op jit(solution)/shard_map/pallas_call | solution.py:591
  13.0 0.0 copy-start
  13.0 0.0 copy-start.4
  13.0 0.0 copy-start.5
  13.0 0.0 copy-start.6
  13.0 11.6 %all-to-all-start.1 = ((f32[128,72,128]{2,1,0:T(8,128)}), f32[128,72,128]{2,1,0:T(8,128)}, u32[]{:S(2)}, u32[]{:S(2)}) async-start(f32[128,72,128]{2,1,0:T(8,128)} %bitcast.51), calls=%async_computation.1 | async-start | bytes 9437184 | tf_op jit(solution)/shard_map/all_to_all | solution.py:607
  24.7 0.0 copy-done
  24.7 0.0 copy-done.4
  24.7 0.0 copy-done.5
  24.7 0.0 copy-done.6
  24.7 9.2 %shard_map.105 = (f32[7176,128]{1,0:T(8,128)}, f32[7176,128]{1,0:T(8,128)}) custom-call(s32[1024]{0:T(1024)S(1)} %bitcast.37, f32[6144,128]{1,0:T(8,128)} %bitcast.45, f32[6144,128]{1,0:T(8,128)} %bitcast.41, f32[6,1024]{1,0:T(8,128)S(1)} %copy-done.4, s32[8,128]{1,0:T(8,128)S(1)} %bitcast.55, f32[8,128]{1,0:T(8,128)S(1)} %bitcast.59), custom_call_target="tpu_custom_call" | custom-call | bytes 14680064 | tf_op jit(solution)/shard_map/pallas_call | solution.py:591
  33.9 49.1 %all-to-all-done.1.recv = f32[128,72,128]{2,1,0:T(8,128)} async-done(((f32[128,72,128]{2,1,0:T(8,128)}), f32[128,72,128]{2,1,0:T(8,128)}, u32[]{:S(2)}, u32[]{:S(2)}) %all-to-all-start.1) | async-done | bytes 4718624 | tf_op jit(solution)/shard_map/all_to_all | solution.py:607
  83.0 0.0 copy-start.1
  83.0 0.0 copy-start.8
  83.0 3.3 %shard_map.106 = f32[1024,128]{1,0:T(8,128)} custom-call(s32[256]{0:T(256)S(1)} %get-tuple-element.67.plan, f32[128,72,128]{2,1,0:T(8,128)} %all-to-all-done.1.recv, f32[7176,128]{1,0:T(8,128)} %get-tuple-element.69.prepared.rows_in), custom_call_target="tpu_custom_call" | custom-call | bytes 2097152 | tf_op jit(solution)/shard_map/pallas_call | solution.py:591
  86.3 4.6 %all-to-all-start.2 = ((f32[128,8,128]{2,1,0:T(8,128)}), f32[128,8,128]{2,1,0:T(8,128)S(1)}, u32[]{:S(2)}, u32[]{:S(2)}) async-start(f32[128,8,128]{2,1,0:T(8,128)} %bitcast.23), calls=%async_computation.2 | async-start | bytes 1048576 | tf_op jit(solution)/shard_map/all_to_all | solution.py:607
  90.9 0.0 copy-done.1
  91.0 0.0 copy-done.8
  91.0 0.0 copy-start.7
  91.0 10.7 %shard_map.107 = (f32[6144,128]{1,0:T(8,128)}, f32[768,128]{1,0:T(8,128)S(1)}, f32[768,128]{1,0:T(8,128)S(1)}) custom-call(s32[8,128]{1,0:T(8,128)S(1)} %bitcast.66, s32[2,128]{1,0:T(2,128)S(1)} %bitcast.38, f32[6144,128]{1,0:T(8,128)} %bitcast.46, f32[7176,128]{1,0:T(8,128)} %get-tuple-element.69.prepared.rows_in, f32[128,72,128]{2,1,0:T(8,128)} %all-to-all-done.1.recv), custom_call_target="tpu_custom_call" | custom-call | flops 1000000000 | bytes 20971520 | tf_op jit(solution)/shard_map/pallas_call | solution.py:591
  101.7 4.9 %collective-permute-start.1 = (f32[768,128]{1,0:T(8,128)S(1)}, f32[768,128]{1,0:T(8,128)S(1)}, u32[]{:S(2)}, u32[]{:S(2)}) collective-permute-start(f32[768,128]{1,0:T(8,128)S(1)} %get-tuple-element.73.own_left), channel_id=1, source_target_pairs={{4,0},{8,4},{12,8},{16,12},{20,16},{24,20},{28,24},{32,28},{36,32}... | collective-permute-start | bytes 1179656 | tf_op jit(solution)/shard_map/ppermute | solution.py:678
  106.6 0.0 collective-permute-start
  106.6 0.6 slice.3
  107.8 0.0 all-to-all-done.2
  107.8 0.0 copy-done.7
  107.8 12.0 %conditional.1 = (f32[6144,128]{1,0:T(8,128)}) conditional(s32[]{:T(128)} %bitcast.16, (f32[128,72,128]{2,1,0:T(8,128)}, f32[128,8,128]{2,1,0:T(8,128)S(1)}, s32[8,128]{1,0:T(8,128)S(1)}, s32[256]{0:T(256)S(1)}, s32[8,128]{1,0:T(8,128)S(1)}, /*index=5*/f32[6144,128]{1,0:T(8,128)}, f32[6,1024]{1,0:T(8,128)S(1)}, s32[8,128]{1,0:T(8,128)S(1)}, ...), branch_computations={%region_0.0_spmd, %region_1.0_spmd} | conditional | flops 1000000000 | bytes 62931008 | solution.py:702
  107.9 12.0 %branch_0_fun.1 = f32[6144,128]{1,0:T(8,128)} custom-call(s32[8,128]{1,0:T(8,128)S(1)} %get-tuple-element.27.arriving, s32[256]{0:T(256)S(1)} %get-tuple-element.40.plan, s32[8,128]{1,0:T(8,128)S(1)} %get-tuple-element.41.info, f32[6144,128]{1,0:T(8,128)} %get-tuple-element.42.inc, f32[6,1024]{1,0:T(8,128)S(1)} %get-tuple-element.43.rates, ...), custom_call_target="tpu_custom_call" | custom-call | flops 1000000000 | bytes 20971520 | tf_op jit(solution)/shard_map/cond/branch_0_fun/pallas_call | solution.py:591
  119.9 0.0 collective-permute-done.1.far_right
  119.9 0.0 collective-permute-done.far_left
  119.9 5.6 %shard_map.108 = f32[6144,128]{1,0:T(8,128)} custom-call(s32[2,128]{1,0:T(2,128)S(1)} %bitcast.39, f32[6144,128]{1,0:T(8,128)} %get-tuple-element.72.column, f32[768,128]{1,0:T(8,128)S(1)} %get-tuple-element.73.own_left, f32[768,128]{1,0:T(8,128)S(1)} %get-tuple-element.74.own_right, f32[768,128]{1,0:T(8,128)S(1)} %collective-permute-done.far_left, ...), custom_call_target="tpu_custom_call" | custom-call | bytes 8388608 | tf_op jit(solution)/shard_map/pallas_call | solution.py:591
Async XLA Ops:
  13.0 11.7 %copy-start = (s32[1,1024]{1,0:T(1,128)S(1)}, s32[1,1024]{1,0:T(1,128)}, u32[]{:S(2)}) copy-start(s32[1,1024]{1,0:T(1,128)} %param.18) | copy-start | bytes 12292
  13.0 11.7 %copy-start.4 = (f32[6,1024]{1,0:T(8,128)S(1)}, f32[6,1024]{1,0:T(8,128)}, u32[]{:S(2)}) copy-start(f32[6,1024]{1,0:T(8,128)} %rates.3) | copy-start | bytes 73732
  13.0 11.7 %copy-start.5 = (s32[1024]{0:T(1024)S(1)}, s32[1024]{0:T(1024)}, u32[]{:S(2)}) copy-start(s32[1024]{0:T(1024)} %param.14) | copy-start | bytes 12292
  13.0 11.7 %copy-start.6 = (f32[1024]{0:T(1024)S(1)}, f32[1024]{0:T(1024)}, u32[]{:S(2)}) copy-start(f32[1024]{0:T(1024)} %param.15) | copy-start | bytes 12292
  13.0 70.0 %all-to-all-start.1 = ((f32[128,72,128]{2,1,0:T(8,128)}), f32[128,72,128]{2,1,0:T(8,128)}, u32[]{:S(2)}, u32[]{:S(2)}) async-start(f32[128,72,128]{2,1,0:T(8,128)} %bitcast.51), calls=%async_computation.1 | async-start | bytes 9437184 | tf_op jit(solution)/shard_map/all_to_all | solution.py:607
  83.0 7.9 %copy-start.1 = (s32[1,2,128]{2,1,0:T(2,128)S(1)}, s32[1,2,128]{2,1,0:T(2,128)}, u32[]{:S(2)}) copy-start(s32[1,2,128]{2,1,0:T(2,128)} %param.19) | copy-start | bytes 3076
  83.0 7.9 %copy-start.8 = (s32[1,128,8]{1,2,0:T(8,128)S(1)}, s32[1,128,8]{1,2,0:T(8,128)}, u32[]{:S(2)}) copy-start(s32[1,128,8]{1,2,0:T(8,128)} %param.16) | copy-start | bytes 12292
  86.3 21.5 %all-to-all-start.2 = ((f32[128,8,128]{2,1,0:T(8,128)}), f32[128,8,128]{2,1,0:T(8,128)S(1)}, u32[]{:S(2)}, u32[]{:S(2)}) async-start(f32[128,8,128]{2,1,0:T(8,128)} %bitcast.23), calls=%async_computation.2 | async-start | bytes 1048576 | tf_op jit(solution)/shard_map/all_to_all | solution.py:607
  91.0 16.9 %copy-start.7 = (s32[1,128,8]{1,2,0:T(8,128)S(1)}, s32[1,128,8]{1,2,0:T(8,128)}, u32[]{:S(2)}) copy-start(s32[1,128,8]{1,2,0:T(8,128)} %param.17) | copy-start | bytes 12292
  101.7 18.2 %collective-permute-start.1 = (f32[768,128]{1,0:T(8,128)S(1)}, f32[768,128]{1,0:T(8,128)S(1)}, u32[]{:S(2)}, u32[]{:S(2)}) collective-permute-start(f32[768,128]{1,0:T(8,128)S(1)} %get-tuple-element.73.own_left), channel_id=1, source_target_pairs={{4,0},{8,4},{12,8},{16,12},{20,16},{24,20},{28,24},{32,28},{36,32}... | collective-permute-start | bytes 1179656 | tf_op jit(solution)/shard_map/ppermute | solution.py:678
  106.6 13.3 %collective-permute-start = (f32[768,128]{1,0:T(8,128)S(1)}, f32[768,128]{1,0:T(8,128)S(1)}, u32[]{:S(2)}, u32[]{:S(2)}) collective-permute-start(f32[768,128]{1,0:T(8,128)S(1)} %get-tuple-element.74.own_right), channel_id=1, source_target_pairs={{0,4},{4,8},{8,12},{12,16},{16,20},{20,24},{24,28},{28,32},{32,36}... | collective-permute-start | bytes 1179656 | tf_op jit(solution)/shard_map/ppermute | solution.py:677
